TPU v7x, 256 devices: a whole 4x4x8 slice. The times are simulated.
256 devices in a mesh: seq: 64 (over x, z, core), exp: 4 (over y).
Axes of the slice: x: 4, y: 4, z: 8, core: 2. Of those that a mesh axis runs over, the one named last changes fastest.
Arguments:
- residual: bfloat16 [8192, 2048], P('seq', 'exp'), may hold values from -36 to 36
- queries: bfloat16 [8192, 2048], P('seq', 'exp'), may hold values from -6 to 6
- key_vectors: bfloat16 [8192, 2048], P('seq', 'exp'), may hold values from -6 to 6
- value_vectors: bfloat16 [8192, 2048], P('seq', 'exp'), may hold values from -36 to 36
- head_gain: float32 [2048], P('exp'), may hold values from 0.25 to 1.75
- norm_gain: float32 [2048], replicated, may hold values from 0.25 to 1.75
- routes: int32 [8192, 8], P('seq'), may hold values from 0 to 63, as said below
- route_gates: float32 [8192, 8], P('seq'), may hold values from 0.2 to 1
- expert_in: bfloat16 [64, 2, 2048, 1024], P('seq'), may hold values from -0.125 to 0.125
- expert_out: bfloat16 [64, 1024, 2048], P('seq'), may hold values from -0.1875 to 0.1875
Outputs:
- layer_out: bfloat16 [8192, 2048], P('seq', 'exp')
Inputs may be any that keep to these rules, and one draw needn't show every extreme that they name: `routes`: each row names 8 different experts. In every aligned block of 32 rows no expert is named by more than 6 rows, and the same 10 experts are named by exactly 6 rows in every block.
All inputs are finite; a program needn't handle non-finite values.
Results may differ from a plain program's by a relative error of at most 0.0075.
Values may be sent and summed in bfloat16 or wider, within the bound.
A program may use at most 128 MiB of HBM per device.

v0:
```python
import jax
import jax.numpy as jnp
from jax import lax
from jax.sharding import PartitionSpec as P

HEAD = 128


def prefix(value, axis, combine, identity):
    devices, here = (lax.axis_size(axis), lax.axis_index(axis))
    everything = lax.all_gather(value, axis)
    start = jnp.broadcast_to(jnp.asarray(identity, value.dtype), value.shape)

    def lap(k, before):
        reached = k < here
        new = combine(before, everything[k])
        return jnp.where(reached, new, before)

    return lax.fori_loop(0, devices, lap, start)


def add_states(earlier, latter):
    return earlier + latter


def slot_ids(block_routes, expert_count, capacity):
    row_count, top_count = block_routes.shape
    expert_ids = jnp.arange(expert_count, dtype=jnp.int32)
    onehot = (
        (block_routes[:, :, None] == expert_ids[None, None, :])
        .astype(jnp.int32)
        .reshape(row_count * top_count, expert_count)
    )
    earlier = jnp.cumsum(onehot, axis=0) - onehot
    ranking = jnp.sum(earlier * onehot, axis=1).reshape(row_count, top_count)
    return block_routes * capacity + ranking


def weigh_rows(flat_rows, slots, gates):
    picked = flat_rows[slots.reshape(-1)].reshape(
        slots.shape[0], slots.shape[1], flat_rows.shape[1]
    )
    return jnp.sum(picked.astype(jnp.float32) * gates[:, :, None], axis=1)


def per_device(
    residual,
    queries,
    key_vectors,
    value_vectors,
    head_gain,
    norm_gain,
    routes,
    route_gates,
    expert_in,
    expert_out,
):
    row_count, quarter = residual.shape
    head_count = quarter // HEAD
    query_heads = queries.reshape(row_count, head_count, HEAD)
    key_heads = key_vectors.reshape(row_count, head_count, HEAD)
    value_heads = value_vectors.reshape(row_count, head_count, HEAD)
    group_state = jnp.einsum(
        "thd,the->hde", key_heads, value_heads, preferred_element_type=jnp.float32
    )
    prior_state = prefix(group_state, "seq", add_states, jnp.zeros_like(group_state))
    carried = jnp.einsum(
        "thd,hde->the",
        query_heads.astype(jnp.float32),
        prior_state,
        precision=lax.Precision.HIGHEST,
    )
    positions = jnp.arange(row_count, dtype=jnp.int32)
    causal = (positions[:, None] >= positions[None, :]).astype(jnp.float32)
    scores = (
        jnp.einsum("thd,shd->hts", query_heads, key_heads, preferred_element_type=jnp.float32)
        * causal[None]
    )
    within = jnp.einsum(
        "hts,she->the", scores, value_heads.astype(jnp.float32), precision=lax.Precision.HIGHEST
    )
    raw_output = carried + within
    scaled = raw_output * lax.rsqrt(
        jnp.mean(raw_output * raw_output, axis=-1, keepdims=True) + 1e-06
    )
    attention_out = scaled.reshape(row_count, quarter) * head_gain
    hidden = (residual.astype(jnp.float32) + attention_out).astype(jnp.bfloat16)
    block_rows = lax.all_to_all(hidden, "exp", split_axis=0, concat_axis=1, tiled=True)
    widened = block_rows.astype(jnp.float32)
    normed = (
        widened * lax.rsqrt(jnp.mean(widened * widened, axis=-1, keepdims=True) + 1e-06) * norm_gain
    ).astype(jnp.bfloat16)
    model_width = normed.shape[1]
    part_count = lax.axis_size("exp")
    sub_count = row_count // part_count
    my_index = lax.axis_index("exp")
    expert_count = lax.axis_size("seq") * expert_in.shape[0]
    top_count = routes.shape[1]
    capacity = min(sub_count, max(2, 3 * sub_count * top_count // (2 * expert_count)))
    slot_count = expert_count * capacity
    my_routes = lax.dynamic_slice_in_dim(routes, my_index * sub_count, sub_count, 0)
    my_gates = lax.dynamic_slice_in_dim(route_gates, my_index * sub_count, sub_count, 0)
    my_slots = slot_ids(my_routes, expert_count, capacity)
    columns = jnp.arange(slot_count, dtype=jnp.int32)
    placer = jnp.sum(
        (my_slots[None, :, :] == columns[:, None, None]).astype(jnp.int32), axis=2
    ).astype(jnp.bfloat16)
    outgoing = (
        jnp.dot(placer, normed, preferred_element_type=jnp.float32)
        .astype(jnp.bfloat16)
        .reshape(expert_count, capacity, model_width)
    )
    arrived = lax.all_to_all(outgoing, "seq", split_axis=0, concat_axis=0, tiled=True)
    flat_rows = arrived.reshape(-1, model_width)
    gate_up = jnp.einsum("nd,gdf->gnf", flat_rows, expert_in[0], preferred_element_type=jnp.float32)
    activated = (jax.nn.silu(gate_up[0]) * gate_up[1]).astype(jnp.bfloat16)
    produced = jnp.dot(activated, expert_out[0], preferred_element_type=jnp.float32).astype(
        jnp.bfloat16
    )
    answered = produced.reshape(arrived.shape)
    returned_rows = lax.all_to_all(answered, "seq", split_axis=0, concat_axis=0, tiled=True)
    mixed_rows = weigh_rows(returned_rows.reshape(slot_count, model_width), my_slots, my_gates)
    moe_out = lax.all_to_all(
        mixed_rows.astype(jnp.bfloat16), "exp", split_axis=1, concat_axis=0, tiled=True
    ).astype(mixed_rows.dtype)
    return (hidden.astype(jnp.float32) + moe_out).astype(jnp.bfloat16)


def solution(mesh):
    placed = (
        P("seq", "exp"),
        P("seq", "exp"),
        P("seq", "exp"),
        P("seq", "exp"),
        P("exp"),
        P(),
        P("seq", None),
        P("seq", None),
        P("seq", None, None, None),
        P("seq", None, None),
    )
    return jax.shard_map(
        per_device, mesh=mesh, in_specs=placed, out_specs=P("seq", "exp"), check_vma=False
    )
```

profile of v0, /device:TPU:6, one launch (start us, length us, event | category | flops | bytes accessed | tf_op | source)
XLA Modules:
  0.0 343.2 jit_solution(2517427410882782573)
XLA Ops:
  6.5 1.1 copy.70
  10.7 1.1 convolution_multiply_fusion
  11.8 98.6 %all-gather.3.cloned.1.call-done = f32[256,128,128]{2,1,0:T(8,128)} async-done(((f32[4,128,128]{2,1,0:T(8,128)}), f32[256,128,128]{2,1,0:T(8,128)}) %all-gather.3.cloned.1.call-update) | async-done | bytes 16777232 | tf_op jit(solution)/shard_map/all_gather | solution.py:11
  110.4 68.1 %while.14 = (s32[]{:T(128)}, f32[4,128,128]{2,1,0:T(8,128)S(1)}, s32[]{:T(128)}, f32[64,4,128,128]{3,2,1,0:T(8,128)}, s32[]{:T(128)}, /*index=5*/s32[]{:T(128)}) while((s32[]{:T(128)}, f32[4,128,128]{2,1,0:T(8,128)S(1)}, s32[]{:T(128)}, f32[64,4,128,128]{3,2,1,0:T(8,128)}, s32[]{:T(128)}, /*index=5*/s32[]{:T(128)}) %tuple.38), condition=%wide.region_1.2_spmd.clone, body=%wide.region_0.1_spmd.clone.sunk | while | flops 196612 | bytes 786533 | solution.py:19
  111.5 1.0 add_select_fusion.2
  113.6 1.0 add_select_fusion.2
  115.7 1.0 add_select_fusion.2
  117.8 1.0 add_select_fusion.2
  127.4 1.0 add_select_fusion.2
  129.6 1.0 add_select_fusion.2
  131.7 1.0 add_select_fusion.2
  133.8 1.0 add_select_fusion.2
  135.9 1.0 add_select_fusion.2
  138.1 1.0 add_select_fusion.2
  147.6 1.0 add_select_fusion.2
  149.8 1.0 add_select_fusion.2
  151.9 1.0 add_select_fusion.2
  180.2 4.3 %all-to-all-start = ((bf16[4,32,512]{2,1,0:T(8,128)(2,1)}), bf16[4,32,512]{2,1,0:T(8,128)(2,1)S(1)}, u32[]{:S(2)}, u32[]{:S(2)}) async-start(bf16[4,32,512]{2,1,0:T(8,128)(2,1)} %bitcast.5), calls=%async_computation | async-start | bytes 262144 | tf_op jit(solution)/shard_map/all_to_all | solution.py:88
  184.7 5.8 %all-to-all-done = bf16[4,32,512]{2,1,0:T(8,128)(2,1)S(1)} async-done(((bf16[4,32,512]{2,1,0:T(8,128)(2,1)}), bf16[4,32,512]{2,1,0:T(8,128)(2,1)S(1)}, u32[]{:S(2)}, u32[]{:S(2)}) %all-to-all-start) | async-done | bytes 131104 | tf_op jit(solution)/shard_map/all_to_all | solution.py:88
  190.7 1.8 convolution_convert_fusion
  192.5 2.5 reshape.131
  195.0 57.1 %all_to_all.33 = bf16[64,6,2048]{2,1,0:T(8,128)(2,1)} all-to-all(bf16[64,6,2048]{2,1,0:T(8,128)(2,1)S(1)} %reshape.131), channel_id=1, replica_groups=mesh['seq'=64,'exp'=4] {'seq'}, dimensions={0} | all-to-all | bytes 3145728 | tf_op jit(solution)/shard_map/all_to_all | solution.py:113
  252.1 2.6 reshape.148
  254.7 5.9 %fusion.8 = f32[2,384,1024]{2,1,0:T(8,128)S(1)} fusion(bf16[384,2048,1]{1,0,2:T(8,128)(2,1)S(1)} %reshape.148, bf16[1,2,2048,1024]{3,2,1,0:T(8,128)(2,1)} %param.20), kind=kOutput, calls=%fused_computation.10 | convolution fusion | flops 3221225472 | bytes 13107200 | tf_op jit(solution)/shard_map/nd,gdf->gnf/dot_general | solution.py:115
  260.7 1.9 fusion.4
  262.6 1.6 reshape.133
  264.1 8.5 %all-to-all-start.2 = ((bf16[64,6,2048]{2,1,0:T(8,128)(2,1)}), bf16[64,6,2048]{2,1,0:T(8,128)(2,1)}, u32[]{:S(2)}, u32[]{:S(2)}) async-start(bf16[64,6,2048]{2,1,0:T(8,128)(2,1)} %reshape.133), calls=%async_computation.2 | async-start | bytes 4194304 | tf_op jit(solution)/shard_map/all_to_all | solution.py:121
  272.9 48.6 %all-to-all-done.2 = bf16[64,6,2048]{2,1,0:T(8,128)(2,1)} async-done(((bf16[64,6,2048]{2,1,0:T(8,128)(2,1)}), bf16[64,6,2048]{2,1,0:T(8,128)(2,1)}, u32[]{:S(2)}, u32[]{:S(2)}) %all-to-all-start.2) | async-done | bytes 1572896 | tf_op jit(solution)/shard_map/all_to_all | solution.py:121
  321.4 2.6 reshape.134
  324.0 1.4 gather_fusion
  326.4 8.4 %all_to_all.34 = bf16[32,4,512]{2,0,1:T(8,128)(2,1)S(1)} all-to-all(bf16[32,4,512]{2,0,1:T(8,128)(2,1)S(1)} %bitcast.100), channel_id=1, replica_groups=mesh['seq'=64,'exp'=4] {'exp'}, dimensions={1} | all-to-all | bytes 262144 | tf_op jit(solution)/shard_map/all_to_all | solution.py:123
  334.7 1.6 fusion.16
  (100 shorter events, 59.4 us)
Async XLA Ops:
  6.5 1.1 copy-start
  6.5 103.9 %all-gather.3.cloned.1.call-start = ((), (), s32[]{:S(2)}) async-start(), calls=%async_computation.4 | async-start | bytes 17039360 | tf_op jit(solution)/shard_map/all_gather | solution.py:11
  11.8 166.7 %copy-start.1 = (bf16[128,512]{1,0:T(8,128)(2,1)S(1)}, bf16[128,512]{1,0:T(8,128)(2,1)}, u32[]{:S(2)}) copy-start(bf16[128,512]{1,0:T(8,128)(2,1)} %param.13) | copy-start | bytes 393220
  178.5 1.0 copy-start.2
  178.5 1.0 copy-start.5
  178.9 11.8 %copy-start.3 = (f32[2048]{0:T(1024)S(1)}, f32[2048]{0:T(1024)}, u32[]{:S(2)}) copy-start(f32[2048]{0:T(1024)} %param.17) | copy-start | bytes 24580
  180.2 10.3 %all-to-all-start = ((bf16[4,32,512]{2,1,0:T(8,128)(2,1)}), bf16[4,32,512]{2,1,0:T(8,128)(2,1)S(1)}, u32[]{:S(2)}, u32[]{:S(2)}) async-start(bf16[4,32,512]{2,1,0:T(8,128)(2,1)} %bitcast.5), calls=%async_computation | async-start | bytes 262144 | tf_op jit(solution)/shard_map/all_to_all | solution.py:88
  254.7 6.0 %copy-start.6 = (bf16[1,1024,2048]{2,1,0:T(8,128)(2,1)S(1)}, bf16[1,1024,2048]{2,1,0:T(8,128)(2,1)}, u32[]{:S(2)}) copy-start(bf16[1,1024,2048]{2,1,0:T(8,128)(2,1)} %param.21) | copy-start | bytes 12582916
  264.1 8.6 %copy-start.4 = (f32[128,8]{0,1:T(8,128)S(1)}, f32[128,8]{0,1:T(8,128)}, u32[]{:S(2)}) copy-start(f32[128,8]{0,1:T(8,128)} %param.19) | copy-start | bytes 12292
  264.1 57.3 %all-to-all-start.2 = ((bf16[64,6,2048]{2,1,0:T(8,128)(2,1)}), bf16[64,6,2048]{2,1,0:T(8,128)(2,1)}, u32[]{:S(2)}, u32[]{:S(2)}) async-start(bf16[64,6,2048]{2,1,0:T(8,128)(2,1)} %reshape.133), calls=%async_computation.2 | async-start | bytes 4194304 | tf_op jit(solution)/shard_map/all_to_all | solution.py:121
Sparse Core Ops, SparseCore 0:
  10.1 100.2 all-gather.2
where the time goes:
time: 348 us; the launch traced here: 343 us
  waiting for transfers between devices  153 us (44%)
  other arithmetic  71 us (20%)
  blocking collectives  65.5 us (19%)
  between operations  13.7 us (4%)
  local copies, waits for them, and re-layouts  13.4 us (4%)
  starting transfers between devices  12.7 us (4%)
  matrix products  12.4 us (4%)
    all_gather x1, waiting for transfers between devices, prefix(): everything = lax.all_gather(value, axis)  98.6 us
    select_n x64, other arithmetic, lap(): return jnp.where(reached, new, before)  66.6 us
    all_to_all x1, blocking collectives, per_device(): lax.all_to_all(outgoing, 'seq', split_axis=0, concat_axis=0, tiled=True)  57.1 us
    all_to_all x1, waiting for transfers between devices, per_device(): lax.all_to_all(answered, 'seq', split_axis=0, concat_axis=0, tiled=True)  48.6 us
    all_to_all x1, starting transfers between devices, per_device(): lax.all_to_all(answered, 'seq', split_axis=0, concat_axis=0, tiled=True)  8.46 us
    all_to_all x1, blocking collectives, per_device(): lax.all_to_all(mixed_rows.astype(jnp.bfloat16), 'exp', split_axis=1, conc...  8.36 us
  transfers between devices with their start and end apart: 3, of which 3 were waited for; matrix products, arithmetic and copies ran while one was open for 1% of the time, Pallas kernels for 0%

commit v1 on v0

v1 whole, which is shorter than its diff:
```python
import functools

import jax
import jax.numpy as jnp
from jax import lax
from jax.experimental import pallas as pl
from jax.experimental.pallas import tpu as pltpu
from jax.sharding import PartitionSpec as P

MESH = pl.DeviceIdType.MESH
F32 = jnp.float32
BF16 = jnp.bfloat16

HEAD = 128
XS, ZS, CS, YS = 4, 8, 2, 4
SEQ = XS * ZS * CS
D = 2048
FF = 1024
SUB = 32
CAP = 6
NC = 4
CW = D // NC
PER_Y = NC // YS
GROUP = ZS * CAP
ROWS = XS * CS * GROUP
TILE = 256
PEERS = ((2, 0), (2, 1), (1, 0), (3, 0), (1, 1), (3, 1), (0, 1))


def nt(a, b):
    return lax.dot_general(a, b, (((1,), (1,)), ((), ())), preferred_element_type=F32)


def tn(a, b):
    return lax.dot_general(a, b, (((0,), (0,)), ((), ())), preferred_element_type=F32)


def nn(a, b):
    return jnp.dot(a, b, preferred_element_type=F32)


def halves(value):
    high = value.astype(BF16)
    return high, (value - high.astype(F32)).astype(BF16)


def layer_kernel(
    q_ref, k_ref, v_ref, res_ref, hgain_ref, ngain_ref, routes_ref, gates_ref, win_ref, wout_ref,
    out_ref,
    w1, w2, state, gathered, running, prior, raw, hidden, rows, meta, place, mixhi, mixlo,
    blk, sel, xin, acc, act, yout, ret, part, rs_send, rs_recv, mine, moe,
    w_sem, st_send, st_recv, pr_send, pr_recv, meta_send, meta_recv, y_send, y_recv,
    ag_send, ag_recv, xs_send, xs_recv, loc_sem, rt_send, rt_recv, rs_ssem, rs_rsem, fy_send, fy_recv,
):
    me = lax.axis_index("seq")
    y = lax.axis_index("exp")
    x = me // (ZS * CS)
    z = (me // CS) % ZS
    c = me % CS
    mine_d = x * CS + c

    def seq_id(xx, zz, cc):
        return (xx * ZS + zz) * CS + cc

    def remote(src, dst, ssem, rsem, seq=None, exp=None):
        return pltpu.make_async_remote_copy(
            src_ref=src, dst_ref=dst, send_sem=ssem, recv_sem=rsem,
            device_id=(me if seq is None else seq, y if exp is None else exp),
            device_id_type=MESH,
        )

    pending = []

    def go(copy):
        copy.start()
        pending.append(copy)
        return copy

    weights = []
    for q in range(NC):
        for g in range(2):
            weights.append(pltpu.make_async_copy(
                win_ref.at[0, g, pl.ds(q * CW, CW), :], w1.at[g, q], w_sem.at[0]))
    for q in range(NC):
        weights.append(pltpu.make_async_copy(
            wout_ref.at[0, :, pl.ds(q * CW, CW)], w2.at[q], w_sem.at[1]))
    for copy in weights:
        copy.start()

    barrier = pltpu.get_barrier_semaphore()

    def greet(i, _):
        pl.semaphore_signal(barrier, inc=1, device_id=((me + i) % SEQ, y), device_id_type=MESH)
        return 0

    lax.fori_loop(1, SEQ, greet, 0)
    for j in range(1, YS):
        pl.semaphore_signal(barrier, inc=1, device_id=(me, (y + j) % YS), device_id_type=MESH)

    heads = q_ref.shape[1] // HEAD
    for h in range(heads):
        cols = pl.ds(h * HEAD, HEAD)
        outer = tn(k_ref[:, cols], v_ref[:, cols])
        state[pl.ds(h * 16, 16)] = outer.reshape(16, 8, HEAD)

    lane = lax.broadcasted_iota(jnp.int32, (SUB, 128), 1)
    my_rows = pl.ds(pl.multiple_of(y * SUB, SUB), SUB)
    my_routes = routes_ref[my_rows, :]
    my_gates = gates_ref[my_rows, :]
    onehot = jnp.zeros((SUB, 128), F32)
    gate_lanes = jnp.zeros((SUB, 128), F32)
    for k in range(my_routes.shape[1]):
        route = my_routes[:, k:k + 1]
        onehot = onehot + jnp.where(route == lane, 1.0, 0.0)
        gate_lanes = gate_lanes + jnp.where(route + 64 == lane, my_gates[:, k:k + 1], 0.0)
    earlier = jnp.where(
        lax.broadcasted_iota(jnp.int32, (SUB, SUB), 0) > lax.broadcasted_iota(jnp.int32, (SUB, SUB), 1),
        1.0, 0.0).astype(BF16)
    rank = nn(earlier, onehot.astype(BF16))
    meta[0] = onehot * (rank + 1.0) + gate_lanes

    pl.semaphore_wait(barrier, SEQ - 1 + YS - 1)

    def send_state(i, _):
        for peer in ((me + i) % SEQ, (me + SEQ - i) % SEQ):
            remote(state.at[peer], gathered.at[me], st_send, st_recv, seq=peer).start()
        return 0

    lax.fori_loop(1, SEQ // 2, send_state, 0)
    far = (me + SEQ // 2) % SEQ
    remote(state.at[far], gathered.at[me], st_send, st_recv, seq=far).start()
    gathered[me] = state[me]

    for k in range(1, ZS):
        go(remote(meta.at[0], meta.at[k], meta_send.at[k - 1], meta_recv.at[k - 1],
                  seq=seq_id(x, (z + k) % ZS, c)))

    causal = (lax.broadcasted_iota(jnp.int32, (128, 128), 0)
              >= lax.broadcasted_iota(jnp.int32, (128, 128), 1))
    for h in range(heads):
        cols = pl.ds(h * HEAD, HEAD)
        scores = jnp.where(causal, nt(q_ref[:, cols], k_ref[:, cols]), 0.0)
        high, low = halves(scores)
        raw[:, cols] = nn(high, v_ref[:, cols]) + nn(low, v_ref[:, cols])

    def others(ref):
        return ref.at[pl.ds(0, SEQ - 1)]

    remote(others(state), others(gathered), st_send, st_recv).wait_recv()

    def scan_step(s, total):
        running[s] = total
        return total + gathered[s]

    lax.fori_loop(0, SEQ, scan_step, jnp.zeros((8, HEAD), F32))

    def send_prior(i, _):
        for peer in ((me + i) % SEQ, (me + SEQ - i) % SEQ):
            remote(running.at[peer], prior.at[me], pr_send, pr_recv, seq=peer).start()
        return 0

    lax.fori_loop(1, SEQ // 2, send_prior, 0)
    remote(running.at[far], prior.at[me], pr_send, pr_recv, seq=far).start()
    prior[me] = running[me]

    for copy in pending[:ZS - 1]:
        copy.wait_recv()
    everyone = meta[...].reshape(ZS * SUB, 128)
    meta_hi, meta_lo = halves(everyone)

    def slot_parts(shape, dim):
        index = lax.broadcasted_iota(jnp.int32, shape, dim)
        group = (index * 10923) >> 16
        return group >> 3, group & 7, index - group * 6

    d_of, k_of, r_of = slot_parts((ROWS, 128), 0)
    expert_of = seq_id(d_of >> 1, z, d_of & 1)
    lanes = lax.broadcasted_iota(jnp.int32, (ROWS, 128), 1)
    pick_rank = jnp.where(lanes == expert_of, 1.0, 0.0).astype(BF16)
    pick_gate = jnp.where(lanes == expert_of + 64, 1.0, 0.0).astype(BF16)
    _, k_row, r_row = slot_parts((ROWS, ZS * SUB), 0)
    k_col = lax.broadcasted_iota(jnp.int32, (ROWS, ZS * SUB), 1) >> 5
    found = (nt(pick_rank, meta_hi) == (r_row + 1).astype(F32)) & (k_row == k_col)
    place[...] = jnp.where(found, 1.0, 0.0).astype(BF16)
    _, k_row, r_row = slot_parts((ZS * SUB, ROWS), 1)
    k_col = lax.broadcasted_iota(jnp.int32, (ZS * SUB, ROWS), 0) >> 5
    found = (nt(meta_hi, pick_rank) == (r_row + 1).astype(F32)) & (k_row == k_col)
    mix = jnp.where(found, nt(meta_hi, pick_gate) + nt(meta_lo, pick_gate), 0.0)
    high, low = halves(mix)
    mixhi[...] = high
    mixlo[...] = low
    acc[...] = jnp.zeros(acc.shape, F32)

    remote(others(running), others(prior), pr_send, pr_recv).wait_recv()
    for h in range(heads):
        cols = pl.ds(h * HEAD, HEAD)
        high, low = halves(prior[pl.ds(h * 16, 16)].reshape(HEAD, HEAD))
        total = nn(q_ref[:, cols], high) + nn(q_ref[:, cols], low) + raw[:, cols]
        scale = lax.rsqrt(jnp.mean(total * total, axis=1, keepdims=True) + 1e-6)
        hidden[:, cols] = (res_ref[:, cols].astype(F32) + total * scale * hgain_ref[:, cols]).astype(BF16)

    y_copies = []
    for j in range(1, YS):
        peer = (y + j) % YS
        y_copies.append(go(remote(
            hidden.at[pl.ds(pl.multiple_of(peer * SUB, SUB), SUB), :], rows.at[y],
            y_send.at[j - 1], y_recv.at[j - 1], exp=peer)))
    rows[y] = hidden[my_rows, :]
    for copy in y_copies:
        copy.wait_recv()
    wide = [rows[j].astype(F32) for j in range(YS)]
    square = sum(jnp.sum(w * w, axis=1, keepdims=True) for w in wide)
    scale = lax.rsqrt(square * (1.0 / D) + 1e-6)
    for q in range(NC):
        part_cols = wide[q // PER_Y][:, (q % PER_Y) * CW:(q % PER_Y + 1) * CW]
        blk[q, 0] = (part_cols * scale * ngain_ref[:, q * CW:(q + 1) * CW]).astype(BF16)

    right = seq_id(x, (z + 1) % ZS, c)
    left = seq_id(x, (z + ZS - 1) % ZS, c)
    far_k = ZS // 2
    ag = {}

    def ag_right(q, k):
        ag["r", q, k] = go(remote(blk.at[q, k - 1], blk.at[q, k], ag_send.at[q, k - 1],
                                  ag_recv.at[q, k - 1], seq=right))

    def ag_left(q, k):
        ag["l", q, k] = go(remote(blk.at[q, (ZS - k + 1) % ZS], blk.at[q, ZS - k], ag_send.at[q, ZS - k - 1],
                                  ag_recv.at[q, ZS - k - 1], seq=left))

    def ag_step(q, k):
        if k > 0:
            ag["r", q, k].wait_recv()
        if k < far_k:
            ag_right(q, k + 1)
        if 0 < k < far_k:
            ag["l", q, k].wait_recv()
        if k + 1 < far_k:
            ag_left(q, k + 1)

    xs = {}

    def select(q):
        chosen = nn(place[...], blk[q].reshape(ZS * SUB, CW)).astype(BF16)
        sel[q] = chosen.reshape(XS * CS, GROUP, CW)
        for j, (dx, dc) in enumerate(PEERS):
            xx, cc = (x + dx) % XS, (c + dc) % CS
            xs[q, j] = go(remote(sel.at[q, xx * CS + cc], xin.at[q, mine_d], xs_send.at[q, j],
                                 xs_recv.at[q, j], seq=seq_id(xx, z, cc)))
        own = pltpu.make_async_copy(sel.at[q, mine_d], xin.at[q, mine_d], loc_sem.at[0, q])
        own.start()
        xs[q, "own"] = own

    def expert_up(q):
        if q == 0:
            pltpu.make_async_copy(w1, w1, w_sem.at[0]).wait()
        for j in range(len(PEERS)):
            xs[q, j].wait_recv()
        xs[q, "own"].wait()

        def tile(i, _):
            cols = pl.ds(pl.multiple_of((i % 4) * TILE, TILE), TILE)
            acc[i] += nn(xin[q].reshape(ROWS, CW), w1[i // 4, q, :, cols])
            return 0

        lax.fori_loop(0, 2 * FF // TILE, tile, 0)

    for slot in range(2 * NC + far_k):
        for q in range(NC):
            k = slot - 2 * q
            if 0 <= k <= far_k:
                ag_step(q, k)
        done = slot - far_k
        if done >= 0 and done % 2 == 0 and done // 2 < NC:
            select(done // 2)
            if done // 2 >= 1:
                expert_up(done // 2 - 1)
    expert_up(NC - 1)

    for n in range(FF // TILE):
        gate = acc[n]
        act[:, n * TILE:(n + 1) * TILE] = (gate / (1.0 + jnp.exp(-gate)) * acc[FF // TILE + n]).astype(BF16)

    pltpu.make_async_copy(w2, w2, w_sem.at[1]).wait()
    order = [(i + (y + 1) * PER_Y) % NC for i in range(NC)]
    rt = {}
    for i in range(NC):
        q = order[i]

        def tile(n, _, q=q, i=i):
            cols = pl.ds(pl.multiple_of(n * TILE, TILE), TILE)
            value = nn(act[...], w2[q, :, cols]).astype(BF16)
            yout[i, :, :, cols] = value.reshape(XS * CS, GROUP, TILE)
            return 0

        lax.fori_loop(0, CW // TILE, tile, 0)
        for j, (dx, dc) in enumerate(PEERS):
            xx, cc = (x + dx) % XS, (c + dc) % CS
            rt[i, j] = go(remote(yout.at[i, xx * CS + cc], ret.at[i, mine_d], rt_send.at[i, j],
                                 rt_recv.at[i, j], seq=seq_id(xx, z, cc)))
        own = pltpu.make_async_copy(yout.at[i, mine_d], ret.at[i, mine_d], loc_sem.at[1, i])
        own.start()
        rt[i, "own"] = own

    rs = {}

    def rs_left(i, step):
        k = far_k + 1 - step
        value = part[i, k]
        if step > 1:
            rs["l", i, step - 1].wait_recv()
            value = value + rs_recv[i, step - 2].astype(F32)
        rs_send[i, step - 1] = value.astype(BF16)
        rs["l", i, step] = go(remote(rs_send.at[i, step - 1], rs_recv.at[i, step - 1],
                                     rs_ssem.at[i, step - 1], rs_rsem.at[i, step - 1], seq=left))

    def rs_right(i, step):
        k = far_k + step
        at = far_k + step - 1
        value = part[i, k]
        if step > 1:
            rs["r", i, step - 1].wait_recv()
            value = value + rs_recv[i, at - 1].astype(F32)
        rs_send[i, at] = value.astype(BF16)
        rs["r", i, step] = go(remote(rs_send.at[i, at], rs_recv.at[i, at],
                                     rs_ssem.at[i, at], rs_rsem.at[i, at], seq=right))

    def rs_step(i, step):
        if step == 1:
            for j in range(len(PEERS)):
                rt[i, j].wait_recv()
            rt[i, "own"].wait()
            answers = ret[i].reshape(ROWS, CW)
            part[i] = (nn(mixhi[...], answers) + nn(mixlo[...], answers)).reshape(ZS, SUB, CW)
        if step <= far_k:
            rs_left(i, step)
        if step < far_k:
            rs_right(i, step)
        if step == far_k + 1:
            rs["l", i, far_k].wait_recv()
            rs["r", i, far_k - 1].wait_recv()
            total = (part[i, 0] + rs_recv[i, far_k - 1].astype(F32) + rs_recv[i, ZS - 2].astype(F32)).astype(BF16)
            mine[i] = total
            if i < NC - PER_Y:
                peer = (y + 1 + i // PER_Y) % YS
                rs["y", i] = go(remote(mine.at[i], moe.at[y, i % PER_Y], fy_send.at[i], fy_recv.at[i], exp=peer))
            else:
                moe[y, i % PER_Y] = total

    for slot in range(3 * NC + far_k + 1):
        for i in range(NC):
            step = slot - 3 * i + 1
            if 1 <= step <= far_k + 1:
                rs_step(i, step)

    for i in range(NC - PER_Y):
        rs["y", i].wait_recv()
    for j in range(YS):
        for p in range(PER_Y):
            cols = pl.ds(p * CW, CW)
            sub = pl.ds(j * SUB, SUB)
            out_ref[sub, cols] = (hidden[sub, cols].astype(F32) + moe[j, p].astype(F32)).astype(BF16)

    remote(others(state), others(gathered), st_send, st_recv).wait_send()
    remote(others(running), others(prior), pr_send, pr_recv).wait_send()
    for copy in pending:
        copy.wait_send()


def per_device(residual, queries, key_vectors, value_vectors, head_gain, norm_gain, routes, route_gates,
               expert_in, expert_out):
    vmem = pl.BlockSpec(memory_space=pltpu.VMEM)
    hbm = pl.BlockSpec(memory_space=pl.ANY)
    dma = pltpu.SemaphoreType.DMA
    peers = len(PEERS)
    return pl.pallas_call(
        layer_kernel,
        out_shape=jax.ShapeDtypeStruct(residual.shape, BF16),
        in_specs=[vmem] * 8 + [hbm] * 2,
        out_specs=vmem,
        scratch_shapes=[
            pltpu.VMEM((2, NC, CW, FF), BF16),
            pltpu.VMEM((NC, FF, CW), BF16),
            pltpu.VMEM((SEQ, 8, HEAD), F32),
            pltpu.VMEM((SEQ, 8, HEAD), F32),
            pltpu.VMEM((SEQ, 8, HEAD), F32),
            pltpu.VMEM((SEQ, 8, HEAD), F32),
            pltpu.VMEM(residual.shape, F32),
            pltpu.VMEM(residual.shape, BF16),
            pltpu.VMEM((YS, SUB, D // YS), BF16),
            pltpu.VMEM((ZS, SUB, 128), F32),
            pltpu.VMEM((ROWS, ZS * SUB), BF16),
            pltpu.VMEM((ZS * SUB, ROWS), BF16),
            pltpu.VMEM((ZS * SUB, ROWS), BF16),
            pltpu.VMEM((NC, ZS, SUB, CW), BF16),
            pltpu.VMEM((NC, XS * CS, GROUP, CW), BF16),
            pltpu.VMEM((NC, XS * CS, GROUP, CW), BF16),
            pltpu.VMEM((2 * FF // TILE, ROWS, TILE), F32),
            pltpu.VMEM((ROWS, FF), BF16),
            pltpu.VMEM((NC, XS * CS, GROUP, CW), BF16),
            pltpu.VMEM((NC, XS * CS, GROUP, CW), BF16),
            pltpu.VMEM((NC, ZS, SUB, CW), F32),
            pltpu.VMEM((NC, ZS - 1, SUB, CW), BF16),
            pltpu.VMEM((NC, ZS - 1, SUB, CW), BF16),
            pltpu.VMEM((NC, SUB, CW), BF16),
            pltpu.VMEM((YS, PER_Y, SUB, CW), BF16),
            dma((2,)), dma, dma, dma, dma,
            dma((ZS - 1,)), dma((ZS - 1,)),
            dma((YS - 1,)), dma((YS - 1,)),
            dma((NC, ZS - 1)), dma((NC, ZS - 1)),
            dma((NC, peers)), dma((NC, peers)),
            dma((2, NC)),
            dma((NC, peers)), dma((NC, peers)),
            dma((NC, ZS - 1)), dma((NC, ZS - 1)),
            dma((NC,)), dma((NC,)),
        ],
        compiler_params=pltpu.CompilerParams(
            collective_id=0, has_side_effects=True, vmem_limit_bytes=60 * 1024 * 1024),
        name="layer",
    )(queries, key_vectors, value_vectors, residual, head_gain.reshape(1, -1), norm_gain.reshape(1, -1),
      routes, route_gates, expert_in, expert_out)


def solution(mesh):
    placed = (
        P("seq", "exp"), P("seq", "exp"), P("seq", "exp"), P("seq", "exp"), P("exp"), P(),
        P("seq", None), P("seq", None), P("seq", None, None, None), P("seq", None, None),
    )
    return jax.shard_map(
        per_device, mesh=mesh, in_specs=placed, out_specs=P("seq", "exp"), check_vma=False
    )
```

time: 348 us -> 136 us (0.39); the launches traced: 343 us -> 135 us
  waiting for transfers between devices: 153 us -> 0 us
  Pallas kernels: 0 us -> 131 us
  other arithmetic: 71 us -> 0 us
  blocking collectives: 65.5 us -> 0 us
  between operations: 13.7 us -> 0.01 us
  starting transfers between devices: 12.7 us -> 0 us
  matrix products: 12.4 us -> 0 us
  local copies, waits for them, and re-layouts: 13.4 us -> 4.39 us
    pallas_call x0 -> x1, Pallas kernels: none -> 131 us  [per_device(): pl.pallas_call(layer_kernel, out_shape=jax.ShapeDtypeStruct(residual.shap...]
    all_gather x1 -> x0, waiting for transfers between devices: 98.6 us -> none  [prefix(): everything = lax.all_gather(value, axis)]
    select_n x65 -> x0, other arithmetic: 66.6 us -> none  [the longest x64 66.6 us: lap(): return jnp.where(reached, new, before)]
    all_to_all x2 -> x0, blocking collectives: 65.5 us -> none  [the longest x1 57.1 us: per_device(): lax.all_to_all(outgoing, 'seq', split_axis=0, concat_axis=0, tiled=True)]
    all_to_all x2 -> x0, waiting for transfers between devices: 54.3 us -> none  [the longest x1 48.6 us: per_device(): lax.all_to_all(answered, 'seq', split_axis=0, concat_axis=0, tiled=True)]
    all_to_all x2 -> x0, starting transfers between devices: 12.7 us -> none  [the longest x1 8.46 us: per_device(): lax.all_to_all(answered, 'seq', split_axis=0, concat_axis=0, tiled=True)]
    dot_general x7 -> x0, matrix products: 12.4 us -> none  [the longest x1 5.94 us: per_device(): jnp.einsum('nd,gdf->gnf', flat_rows, expert_in[0], preferred_element_type...]
    reshape x8 -> x0, local copies, waits for them, and re-layouts: 10.6 us -> none  [the longest x1 2.6 us: per_device(): flat_rows = arrived.reshape(-1, model_width)]
  transfers between devices with their start and end apart: 3 -> 0, of which waited for: 3 -> 0; matrix products, arithmetic and copies ran while one was open for 1% -> 0% of each run, Pallas kernels for 0% -> 0%
where the time goes in v1:
time: 136 us; the launch traced here: 135 us
  Pallas kernels  131 us (96%)
  local copies, waits for them, and re-layouts  4.39 us (3%)
    pallas_call x1, Pallas kernels, per_device(): pl.pallas_call(layer_kernel, out_shape=jax.ShapeDtypeStruct(residual.shap...  131 us
    unnamed x3, local copies, waits for them, and re-layouts  4.39 us

profile of v1, /device:TPU:6, one launch (start us, length us, event | category | flops | bytes accessed | tf_op | source)
XLA Modules:
  0.0 135.0 jit_solution(14417373404807990748)
XLA Ops:
  0.0 1.4 %copy.11.routes_ref = s32[128,8]{1,0:T(8,128)} copy(s32[128,8]{0,1:T(8,128)} %param.16) | data formatting | bytes 8192 | tf_op args[6]
  1.4 1.4 %copy.12.gates_ref = f32[128,8]{1,0:T(8,128)} copy(f32[128,8]{0,1:T(8,128)} %param.17) | data formatting | bytes 8192 | tf_op args[7]
  2.8 130.6 %layer.1 = bf16[128,512]{1,0:T(8,128)(2,1)} custom-call(bf16[128,512]{1,0:T(8,128)(2,1)} %q_ref.1, bf16[128,512]{1,0:T(8,128)(2,1)} %k_ref.1, bf16[128,512]{1,0:T(8,128)(2,1)} %v_ref.1, bf16[128,512]{1,0:T(8,128)(2,1)} %res_ref.1, f32[1,512]{1,0:T(1,128)} %bitcast.3, f32[1,2048]{1,0:T(1,128)} %bitcast.2, s32[128,8]{1,0:T(8,128)} %copy.11.routes_ref, ...), custom_call_target="tpu_custom_call" | custom-call | tf_op jit(solution)/shard_map/layer/pallas_call | solution.py:376
  133.5 1.6 %copy.14 = bf16[128,512]{1,0:T(8,128)(2,1)} copy(bf16[128,512]{1,0:T(8,128)(2,1)} %layer.1) | data formatting | bytes 262144

commit v2 on v1

v2 whole, which is shorter than its diff:
```python
import functools

import jax
import jax.numpy as jnp
from jax import lax
from jax.experimental import pallas as pl
from jax.experimental.pallas import tpu as pltpu
from jax.sharding import PartitionSpec as P

MESH = pl.DeviceIdType.MESH
F32 = jnp.float32
BF16 = jnp.bfloat16

HEAD = 128
XS, ZS, CS, YS = 4, 8, 2, 4
SEQ = XS * ZS * CS
D = 2048
FF = 1024
SUB = 32
CAP = 6
NC = 4
CW = D // NC
PER_Y = NC // YS
HALF = ZS // 2
GROUP = HALF * CAP
HROWS = XS * CS * GROUP
ROWS = 2 * HROWS
TILE = 256
PEERS = ((2, 0), (2, 1), (1, 0), (3, 0), (1, 1), (3, 1), (0, 1))


def nt(a, b):
    return lax.dot_general(a, b, (((1,), (1,)), ((), ())), preferred_element_type=F32)


def tn(a, b):
    return lax.dot_general(a, b, (((0,), (0,)), ((), ())), preferred_element_type=F32)


def nn(a, b):
    return jnp.dot(a, b, preferred_element_type=F32)


def halves(value):
    high = value.astype(BF16)
    return high, (value - high.astype(F32)).astype(BF16)


def layer_kernel(
    q_ref, k_ref, v_ref, res_ref, hgain_ref, ngain_ref, routes_ref, gates_ref, win_ref, wout_ref,
    out_ref,
    w1, w2, state, gathered, running, prior, raw, hidden, rows, meta, place, mixhi, mixlo,
    blk, sel, xin, acc, act, yout, ret, part, rs_send, rs_recv, mine, moe,
    w_sem, st_send, st_recv, pr_send, pr_recv, meta_send, meta_recv, y_send, y_recv,
    ag_send, ag_recv, xs_send, xs_recv, loc_sem, rt_send, rt_recv, rs_ssem, rs_rsem, fy_send, fy_recv,
):
    me = lax.axis_index("seq")
    y = lax.axis_index("exp")
    x = me // (ZS * CS)
    z = (me // CS) % ZS
    c = me % CS
    mine_d = x * CS + c

    def seq_id(xx, zz, cc):
        return (xx * ZS + zz) * CS + cc

    def remote(src, dst, ssem, rsem, seq=None, exp=None):
        return pltpu.make_async_remote_copy(
            src_ref=src, dst_ref=dst, send_sem=ssem, recv_sem=rsem,
            device_id=(me if seq is None else seq, y if exp is None else exp),
            device_id_type=MESH,
        )

    pending = []

    def go(copy):
        copy.start()
        pending.append(copy)
        return copy

    weights = []
    for q in range(NC):
        for g in range(2):
            weights.append(pltpu.make_async_copy(
                win_ref.at[0, g, pl.ds(q * CW, CW), :], w1.at[g, q], w_sem.at[0]))
    for q in range(NC):
        weights.append(pltpu.make_async_copy(
            wout_ref.at[0, :, pl.ds(q * CW, CW)], w2.at[q], w_sem.at[1]))
    for copy in weights:
        copy.start()

    barrier = pltpu.get_barrier_semaphore()

    def greet(i, _):
        pl.semaphore_signal(barrier, inc=1, device_id=((me + i) % SEQ, y), device_id_type=MESH)
        return 0

    lax.fori_loop(1, SEQ, greet, 0)
    for j in range(1, YS):
        pl.semaphore_signal(barrier, inc=1, device_id=(me, (y + j) % YS), device_id_type=MESH)

    heads = q_ref.shape[1] // HEAD
    for h in range(heads):
        cols = pl.ds(h * HEAD, HEAD)
        outer = tn(k_ref[:, cols], v_ref[:, cols])
        state[pl.ds(h * 16, 16)] = outer.reshape(16, 8, HEAD).astype(BF16)

    pl.semaphore_wait(barrier, SEQ - 1 + YS - 1)

    def send_state(i, _):
        for peer in ((me + i) % SEQ, (me + SEQ - i) % SEQ):
            remote(state.at[peer], gathered.at[me], st_send, st_recv, seq=peer).start()
        return 0

    lax.fori_loop(1, SEQ // 2, send_state, 0)
    far = (me + SEQ // 2) % SEQ
    remote(state.at[far], gathered.at[me], st_send, st_recv, seq=far).start()
    gathered[me] = state[me]

    tok = lax.broadcasted_iota(jnp.int32, (128, 128), 1)
    row = lax.broadcasted_iota(jnp.int32, (128, 128), 0)
    onehot = jnp.zeros((128, 128), F32)
    gate_rows = jnp.zeros((128, 128), F32)
    for k in range(routes_ref.shape[0]):
        route = routes_ref[k:k + 1, :]
        onehot = onehot + jnp.where(route == row, 1.0, 0.0)
        gate_rows = gate_rows + jnp.where(route + 64 == row, gates_ref[k:k + 1, :], 0.0)
    earlier = jnp.where((row < tok) & ((row >> 5) == (tok >> 5)), 1.0, 0.0).astype(BF16)
    table = onehot * (nn(onehot.astype(BF16), earlier) + 1.0) + gate_rows
    take = jnp.where(
        lax.broadcasted_iota(jnp.int32, (SUB, 128), 1) == lax.broadcasted_iota(jnp.int32, (SUB, 128), 0) + y * SUB,
        1.0, 0.0).astype(BF16)
    high, low = halves(table)
    meta[1] = nt(take, high) + nt(take, low)
    for k in range(1, ZS):
        go(remote(meta.at[1], meta.at[(k + 1) % ZS], meta_send.at[k - 1], meta_recv.at[k - 1],
                  seq=seq_id(x, (z + k) % ZS, c)))

    causal = row >= tok
    for h in range(heads):
        cols = pl.ds(h * HEAD, HEAD)
        scores = jnp.where(causal, nt(q_ref[:, cols], k_ref[:, cols]), 0.0)
        high, low = halves(scores)
        raw[:, cols] = nn(high, v_ref[:, cols]) + nn(low, v_ref[:, cols])

    def others(ref):
        return ref.at[pl.ds(0, SEQ - 1)]

    remote(others(state), others(gathered), st_send, st_recv).wait_recv()

    def scan_step(s, total):
        running[s] = total.astype(BF16)
        return total + gathered[s].astype(F32)

    lax.fori_loop(0, SEQ, scan_step, jnp.zeros((8, HEAD), F32))

    def send_prior(i, _):
        for peer in ((me + i) % SEQ, (me + SEQ - i) % SEQ):
            remote(running.at[peer], prior.at[me], pr_send, pr_recv, seq=peer).start()
        return 0

    lax.fori_loop(1, SEQ // 2, send_prior, 0)
    remote(running.at[far], prior.at[me], pr_send, pr_recv, seq=far).start()
    prior[me] = running[me]

    for copy in pending[:ZS - 1]:
        copy.wait_recv()
    everyone = meta[...].reshape(ZS * SUB, 128)
    meta_hi, meta_lo = halves(everyone)

    def slot_parts(shape, dim):
        index = lax.broadcasted_iota(jnp.int32, shape, dim)
        group = (index * 10923) >> 16
        return group >> 2, group & 3, index - group * CAP

    d_of, _, _ = slot_parts((HROWS, 128), 0)
    expert_of = seq_id(d_of >> 1, z, d_of & 1)
    lanes = lax.broadcasted_iota(jnp.int32, (HROWS, 128), 1)
    pick_rank = jnp.where(lanes == expert_of, 1.0, 0.0).astype(BF16)
    pick_gate = jnp.where(lanes == expert_of + 64, 1.0, 0.0).astype(BF16)
    _, k_row, r_row = slot_parts((HROWS, 128), 0)
    k_col = lanes >> 5
    _, mk_row, mr_row = slot_parts((128, HROWS), 1)
    mk_col = lax.broadcasted_iota(jnp.int32, (128, HROWS), 0) >> 5
    for hf in range(2):
        hi_part, lo_part = meta_hi[hf * 128:(hf + 1) * 128], meta_lo[hf * 128:(hf + 1) * 128]
        found = (nt(pick_rank, hi_part) == (r_row + 1).astype(F32)) & (k_row == k_col)
        place[hf] = jnp.where(found, 1.0, 0.0).astype(BF16)
        found = (nt(hi_part, pick_rank) == (mr_row + 1).astype(F32)) & (mk_row == mk_col)
        mix = jnp.where(found, nt(hi_part, pick_gate) + nt(lo_part, pick_gate), 0.0)
        high, low = halves(mix)
        mixhi[hf] = high
        mixlo[hf] = low
    acc[...] = jnp.zeros(acc.shape, F32)

    remote(others(running), others(prior), pr_send, pr_recv).wait_recv()
    for h in range(heads):
        cols = pl.ds(h * HEAD, HEAD)
        before = prior[pl.ds(h * 16, 16)].astype(F32).reshape(HEAD, HEAD).astype(BF16)
        total = nn(q_ref[:, cols], before) + raw[:, cols]
        scale = lax.rsqrt(jnp.mean(total * total, axis=1, keepdims=True) + 1e-6)
        hidden[:, cols] = (res_ref[:, cols].astype(F32) + total * scale * hgain_ref[:, cols]).astype(BF16)

    y_copies = []
    for j in range(1, YS):
        peer = (y + j) % YS
        y_copies.append(go(remote(
            hidden.at[pl.ds(pl.multiple_of(peer * SUB, SUB), SUB), :], rows.at[y],
            y_send.at[j - 1], y_recv.at[j - 1], exp=peer)))
    rows[y] = hidden[pl.ds(pl.multiple_of(y * SUB, SUB), SUB), :]
    for copy in y_copies:
        copy.wait_recv()
    wide = [rows[j].astype(F32) for j in range(YS)]
    square = sum(jnp.sum(w * w, axis=1, keepdims=True) for w in wide)
    scale = lax.rsqrt(square * (1.0 / D) + 1e-6)
    for q in range(NC):
        part_cols = wide[q // PER_Y][:, (q % PER_Y) * CW:(q % PER_Y + 1) * CW]
        blk[q, 1] = (part_cols * scale * ngain_ref[:, q * CW:(q + 1) * CW]).astype(BF16)

    right = seq_id(x, (z + 1) % ZS, c)
    left = seq_id(x, (z + ZS - 1) % ZS, c)
    far_k = ZS // 2
    ag = {}

    def at(k):
        return (k + 1) % ZS

    def ag_right(q, k):
        ag["r", q, k] = go(remote(blk.at[q, at(k - 1)], blk.at[q, at(k)], ag_send.at[q, k - 1],
                                  ag_recv.at[q, k - 1], seq=right))

    def ag_left(q, k):
        ag["l", q, k] = go(remote(blk.at[q, at(ZS - k + 1)], blk.at[q, at(ZS - k)], ag_send.at[q, ZS - k - 1],
                                  ag_recv.at[q, ZS - k - 1], seq=left))

    def ag_step(q, k):
        if k > 0:
            ag["r", q, k].wait_recv()
        if k < far_k:
            ag_right(q, k + 1)
        if 0 < k < far_k:
            ag["l", q, k].wait_recv()
        if k + 1 < far_k:
            ag_left(q, k + 1)

    xs = {}

    def select(q, hf):
        source = blk[q, hf * HALF:(hf + 1) * HALF].reshape(HALF * SUB, CW)
        sel[q, hf] = nn(place[hf], source).astype(BF16).reshape(XS * CS, GROUP, CW)
        for j, (dx, dc) in enumerate(PEERS):
            xx, cc = (x + dx) % XS, (c + dc) % CS
            xs[q, hf, j] = go(remote(sel.at[q, hf, xx * CS + cc], xin.at[q, hf, mine_d], xs_send.at[q, hf, j],
                                     xs_recv.at[q, hf, j], seq=seq_id(xx, z, cc)))
        own = pltpu.make_async_copy(sel.at[q, hf, mine_d], xin.at[q, hf, mine_d], loc_sem.at[0, q, hf])
        own.start()
        xs[q, hf, "own"] = own

    def expert_up(q):
        if q == 0:
            pltpu.make_async_copy(w1, w1, w_sem.at[0]).wait()
        for hf in range(2):
            for j in range(len(PEERS)):
                xs[q, hf, j].wait_recv()
            xs[q, hf, "own"].wait()

        def tile(i, _):
            cols = pl.ds(pl.multiple_of((i % 4) * TILE, TILE), TILE)
            acc[i] += nn(xin[q].reshape(ROWS, CW), w1[i // 4, q, :, cols])
            return 0

        lax.fori_loop(0, 2 * FF // TILE, tile, 0)

    for q in range(NC):
        ag_step(q, 0)
    for k in range(1, far_k + 1):
        for q in range(NC):
            ag_step(q, k)
            if k == 2:
                select(q, 0)
            if k == far_k:
                select(q, 1)
    for q in range(NC):
        expert_up(q)

    for n in range(FF // TILE):
        gate = acc[n]
        act[:, n * TILE:(n + 1) * TILE] = (gate / (1.0 + jnp.exp(-gate)) * acc[FF // TILE + n]).astype(BF16)

    pltpu.make_async_copy(w2, w2, w_sem.at[1]).wait()
    order = [(i + (y + 1) * PER_Y) % NC for i in range(NC)]
    rt = {}

    def send_back(i, hf):
        for j, (dx, dc) in enumerate(PEERS):
            xx, cc = (x + dx) % XS, (c + dc) % CS
            rt[i, hf, j] = go(remote(yout.at[i, hf, xx * CS + cc], ret.at[i, hf, mine_d], rt_send.at[i, hf, j],
                                     rt_recv.at[i, hf, j], seq=seq_id(xx, z, cc)))
        own = pltpu.make_async_copy(yout.at[i, hf, mine_d], ret.at[i, hf, mine_d], loc_sem.at[1, i, hf])
        own.start()
        rt[i, hf, "own"] = own

    for i in range(NC):
        q = order[i]

        def tile(n, _, q=q, i=i):
            cols = pl.ds(pl.multiple_of(n * TILE, TILE), TILE)
            value = nn(act[...], w2[q, :, cols]).astype(BF16)
            yout[i, :, :, :, cols] = value.reshape(2, XS * CS, GROUP, TILE)
            return 0

        lax.fori_loop(0, CW // TILE, tile, 0)
        send_back(i, 1)
    for i in range(NC):
        send_back(i, 0)

    rs = {}

    def answers(i, hf):
        for j in range(len(PEERS)):
            rt[i, hf, j].wait_recv()
        rt[i, hf, "own"].wait()
        value = ret[i, hf].reshape(HROWS, CW)
        part[i, hf] = (nn(mixhi[hf], value) + nn(mixlo[hf], value)).reshape(HALF, SUB, CW)

    def own_part(i, k):
        return part[i, at(k) // HALF, at(k) % HALF]

    def rs_left(i, step):
        value = own_part(i, far_k + 1 - step)
        if step > 1:
            rs["l", i, step - 1].wait_recv()
            value = value + rs_recv[i, step - 2].astype(F32)
        rs_send[i, step - 1] = value.astype(BF16)
        rs["l", i, step] = go(remote(rs_send.at[i, step - 1], rs_recv.at[i, step - 1],
                                     rs_ssem.at[i, step - 1], rs_rsem.at[i, step - 1], seq=left))

    def rs_right(i, step):
        slot = far_k + step - 1
        value = own_part(i, far_k + step)
        if step > 1:
            rs["r", i, step - 1].wait_recv()
            value = value + rs_recv[i, slot - 1].astype(F32)
        rs_send[i, slot] = value.astype(BF16)
        rs["r", i, step] = go(remote(rs_send.at[i, slot], rs_recv.at[i, slot],
                                     rs_ssem.at[i, slot], rs_rsem.at[i, slot], seq=right))

    def rs_step(i, step):
        if step == 1:
            answers(i, 1)
        if step == 3:
            answers(i, 0)
        if step <= far_k:
            rs_left(i, step)
        if step < far_k:
            rs_right(i, step)
        if step == far_k + 1:
            rs["l", i, far_k].wait_recv()
            rs["r", i, far_k - 1].wait_recv()
            total = (own_part(i, 0) + rs_recv[i, far_k - 1].astype(F32) + rs_recv[i, ZS - 2].astype(F32)).astype(BF16)
            mine[i] = total
            if i < NC - PER_Y:
                peer = (y + 1 + i // PER_Y) % YS
                rs["y", i] = go(remote(mine.at[i], moe.at[y, i % PER_Y], fy_send.at[i], fy_recv.at[i], exp=peer))
            else:
                moe[y, i % PER_Y] = total

    spacing = 8.8 / NC
    events = []
    for i in range(NC):
        first, second = spacing * (i + 1), spacing * (NC + i + 1)
        for step, when in ((1, first), (2, first + 2.8), (3, second), (4, second + 2.8), (5, second + 5.6)):
            events.append((when, i, step))
    for when, i, step in sorted(events):
        rs_step(i, step)

    for i in range(NC - PER_Y):
        rs["y", i].wait_recv()
    for j in range(YS):
        for p in range(PER_Y):
            cols = pl.ds(p * CW, CW)
            sub = pl.ds(j * SUB, SUB)
            out_ref[sub, cols] = (hidden[sub, cols].astype(F32) + moe[j, p].astype(F32)).astype(BF16)

    remote(others(state), others(gathered), st_send, st_recv).wait_send()
    remote(others(running), others(prior), pr_send, pr_recv).wait_send()
    for copy in pending:
        copy.wait_send()


def per_device(residual, queries, key_vectors, value_vectors, head_gain, norm_gain, routes, route_gates,
               expert_in, expert_out):
    vmem = pl.BlockSpec(memory_space=pltpu.VMEM)
    hbm = pl.BlockSpec(memory_space=pl.ANY)
    dma = pltpu.SemaphoreType.DMA
    peers = len(PEERS)
    return pl.pallas_call(
        layer_kernel,
        out_shape=jax.ShapeDtypeStruct(residual.shape, BF16),
        in_specs=[vmem] * 8 + [hbm] * 2,
        out_specs=vmem,
        scratch_shapes=[
            pltpu.VMEM((2, NC, CW, FF), BF16),
            pltpu.VMEM((NC, FF, CW), BF16),
            pltpu.VMEM((SEQ, 8, HEAD), BF16),
            pltpu.VMEM((SEQ, 8, HEAD), BF16),
            pltpu.VMEM((SEQ, 8, HEAD), BF16),
            pltpu.VMEM((SEQ, 8, HEAD), BF16),
            pltpu.VMEM(residual.shape, F32),
            pltpu.VMEM(residual.shape, BF16),
            pltpu.VMEM((YS, SUB, D // YS), BF16),
            pltpu.VMEM((ZS, SUB, 128), F32),
            pltpu.VMEM((2, HROWS, HALF * SUB), BF16),
            pltpu.VMEM((2, HALF * SUB, HROWS), BF16),
            pltpu.VMEM((2, HALF * SUB, HROWS), BF16),
            pltpu.VMEM((NC, ZS, SUB, CW), BF16),
            pltpu.VMEM((NC, 2, XS * CS, GROUP, CW), BF16),
            pltpu.VMEM((NC, 2, XS * CS, GROUP, CW), BF16),
            pltpu.VMEM((2 * FF // TILE, ROWS, TILE), F32),
            pltpu.VMEM((ROWS, FF), BF16),
            pltpu.VMEM((NC, 2, XS * CS, GROUP, CW), BF16),
            pltpu.VMEM((NC, 2, XS * CS, GROUP, CW), BF16),
            pltpu.VMEM((NC, 2, HALF, SUB, CW), F32),
            pltpu.VMEM((NC, ZS - 1, SUB, CW), BF16),
            pltpu.VMEM((NC, ZS - 1, SUB, CW), BF16),
            pltpu.VMEM((NC, SUB, CW), BF16),
            pltpu.VMEM((YS, PER_Y, SUB, CW), BF16),
            dma((2,)), dma, dma, dma, dma,
            dma((ZS - 1,)), dma((ZS - 1,)),
            dma((YS - 1,)), dma((YS - 1,)),
            dma((NC, ZS - 1)), dma((NC, ZS - 1)),
            dma((NC, 2, peers)), dma((NC, 2, peers)),
            dma((2, NC, 2)),
            dma((NC, 2, peers)), dma((NC, 2, peers)),
            dma((NC, ZS - 1)), dma((NC, ZS - 1)),
            dma((NC,)), dma((NC,)),
        ],
        compiler_params=pltpu.CompilerParams(
            collective_id=0, has_side_effects=True, vmem_limit_bytes=60 * 1024 * 1024),
        name="layer",
    )(queries, key_vectors, value_vectors, residual, head_gain.reshape(1, -1), norm_gain.reshape(1, -1),
      routes.T, route_gates.T, expert_in, expert_out)


def solution(mesh):
    placed = (
        P("seq", "exp"), P("seq", "exp"), P("seq", "exp"), P("seq", "exp"), P("exp"), P(),
        P("seq", None), P("seq", None), P("seq", None, None, None), P("seq", None, None),
    )
    return jax.shard_map(
        per_device, mesh=mesh, in_specs=placed, out_specs=P("seq", "exp"), check_vma=False
    )
```

time: 136 us -> 95.4 us (0.70)
  Pallas kernels: 131 us -> 93.7 us
  local copies, waits for them, and re-layouts: 4.39 us -> 1.57 us
    pallas_call x1, Pallas kernels: 131 us -> 93.7 us  [per_device(): pl.pallas_call(layer_kernel, out_shape=jax.ShapeDtypeStruct(residual.shap...]
    unnamed x3 -> x1, local copies, waits for them, and re-layouts: 4.39 us -> 1.57 us
where the time goes in v2:
time: 95.4 us; the launch traced here: 95.3 us
  Pallas kernels  93.7 us (98%)
  local copies, waits for them, and re-layouts  1.57 us (2%)
    pallas_call x1, Pallas kernels, per_device(): pl.pallas_call(layer_kernel, out_shape=jax.ShapeDtypeStruct(residual.shap...  93.7 us

profile of v2, /device:TPU:6, one launch (start us, length us, event | category | flops | bytes accessed | tf_op | source)
XLA Modules:
  0.0 95.3 jit_solution(15676029587395898116)
XLA Ops:
  0.0 93.7 %layer.1 = bf16[128,512]{1,0:T(8,128)(2,1)} custom-call(bf16[128,512]{1,0:T(8,128)(2,1)} %q_ref.1, bf16[128,512]{1,0:T(8,128)(2,1)} %k_ref.1, bf16[128,512]{1,0:T(8,128)(2,1)} %v_ref.1, bf16[128,512]{1,0:T(8,128)(2,1)} %res_ref.1, f32[1,512]{1,0:T(1,128)} %bitcast.7, f32[1,2048]{1,0:T(1,128)} %bitcast.4, s32[8,128]{1,0:T(8,128)} %bitcast.5, ...), custom_call_target="tpu_custom_call" | custom-call | tf_op jit(solution)/shard_map/layer/pallas_call | solution.py:397
  93.7 1.6 %copy.12 = bf16[128,512]{1,0:T(8,128)(2,1)} copy(bf16[128,512]{1,0:T(8,128)(2,1)} %layer.1) | data formatting | bytes 262144

commit v3 on v2

--- a/solution.py
+++ b/solution.py
@@ -191,7 +191,6 @@
         high, low = halves(mix)
         mixhi[hf] = high
         mixlo[hf] = low
-    acc[...] = jnp.zeros(acc.shape, F32)
 
     remote(others(running), others(prior), pr_send, pr_recv).wait_recv()
     for h in range(heads):
@@ -256,20 +255,45 @@
         own.start()
         xs[q, hf, "own"] = own
 
-    def expert_up(q):
-        if q == 0:
+    def expert_up(q, hf):
+        if q == 0 and hf == 0:
             pltpu.make_async_copy(w1, w1, w_sem.at[0]).wait()
-        for hf in range(2):
-            for j in range(len(PEERS)):
-                xs[q, hf, j].wait_recv()
-            xs[q, hf, "own"].wait()
+        for j in range(len(PEERS)):
+            xs[q, hf, j].wait_recv()
+        xs[q, hf, "own"].wait()
 
         def tile(i, _):
             cols = pl.ds(pl.multiple_of((i % 4) * TILE, TILE), TILE)
-            acc[i] += nn(xin[q].reshape(ROWS, CW), w1[i // 4, q, :, cols])
+            value = nn(xin[q, hf].reshape(HROWS, CW), w1[i // 4, q, :, cols])
+            if q == 0:
+                acc[hf, i] = value
+            else:
+                acc[hf, i] += value
             return 0
 
-        lax.fori_loop(0, 2 * FF // TILE, tile, 0)
+        lax.fori_loop(0, 2 * FF // TILE, tile, 0, unroll=2)
+
+    def activate(hf):
+        for n in range(FF // TILE):
+            gate = acc[hf, n]
+            act[hf, :, n * TILE:(n + 1) * TILE] = (
+                gate / (1.0 + jnp.exp(-gate)) * acc[hf, FF // TILE + n]).astype(BF16)
+
+    rt = {}
+    order = [(i + (y + 1) * PER_Y) % NC for i in range(NC)]
+
+    def expert_down(i, hf):
+        for n in range(CW // TILE):
+            cols = pl.ds(n * TILE, TILE)
+            value = nn(act[hf], w2[order[i], :, cols]).astype(BF16)
+            yout[i, hf, :, :, cols] = value.reshape(XS * CS, GROUP, TILE)
+        for j, (dx, dc) in enumerate(PEERS):
+            xx, cc = (x + dx) % XS, (c + dc) % CS
+            rt[i, hf, j] = go(remote(yout.at[i, hf, xx * CS + cc], ret.at[i, hf, mine_d], rt_send.at[i, hf, j],
+                                     rt_recv.at[i, hf, j], seq=seq_id(xx, z, cc)))
+        own = pltpu.make_async_copy(yout.at[i, hf, mine_d], ret.at[i, hf, mine_d], loc_sem.at[1, i, hf])
+        own.start()
+        rt[i, hf, "own"] = own
 
     for q in range(NC):
         ag_step(q, 0)
@@ -281,38 +305,18 @@
             if k == far_k:
                 select(q, 1)
     for q in range(NC):
-        expert_up(q)
-
-    for n in range(FF // TILE):
-        gate = acc[n]
-        act[:, n * TILE:(n + 1) * TILE] = (gate / (1.0 + jnp.exp(-gate)) * acc[FF // TILE + n]).astype(BF16)
-
+        expert_up(q, 0)
+    activate(0)
     pltpu.make_async_copy(w2, w2, w_sem.at[1]).wait()
-    order = [(i + (y + 1) * PER_Y) % NC for i in range(NC)]
-    rt = {}
-
-    def send_back(i, hf):
-        for j, (dx, dc) in enumerate(PEERS):
-            xx, cc = (x + dx) % XS, (c + dc) % CS
-            rt[i, hf, j] = go(remote(yout.at[i, hf, xx * CS + cc], ret.at[i, hf, mine_d], rt_send.at[i, hf, j],
-                                     rt_recv.at[i, hf, j], seq=seq_id(xx, z, cc)))
-        own = pltpu.make_async_copy(yout.at[i, hf, mine_d], ret.at[i, hf, mine_d], loc_sem.at[1, i, hf])
-        own.start()
-        rt[i, hf, "own"] = own
-
+    for i in range(NC // 2):
+        expert_down(i, 0)
+    for q in range(NC):
+        expert_up(q, 1)
+    activate(1)
     for i in range(NC):
-        q = order[i]
-
-        def tile(n, _, q=q, i=i):
-            cols = pl.ds(pl.multiple_of(n * TILE, TILE), TILE)
-            value = nn(act[...], w2[q, :, cols]).astype(BF16)
-            yout[i, :, :, :, cols] = value.reshape(2, XS * CS, GROUP, TILE)
-            return 0
-
-        lax.fori_loop(0, CW // TILE, tile, 0)
-        send_back(i, 1)
-    for i in range(NC):
-        send_back(i, 0)
+        expert_down(i, 1)
+    for i in range(NC // 2, NC):
+        expert_down(i, 0)
 
     rs = {}
 
@@ -326,53 +330,53 @@
     def own_part(i, k):
         return part[i, at(k) // HALF, at(k) % HALF]
 
-    def rs_left(i, step):
-        value = own_part(i, far_k + 1 - step)
-        if step > 1:
-            rs["l", i, step - 1].wait_recv()
-            value = value + rs_recv[i, step - 2].astype(F32)
-        rs_send[i, step - 1] = value.astype(BF16)
-        rs["l", i, step] = go(remote(rs_send.at[i, step - 1], rs_recv.at[i, step - 1],
-                                     rs_ssem.at[i, step - 1], rs_rsem.at[i, step - 1], seq=left))
-
-    def rs_right(i, step):
-        slot = far_k + step - 1
-        value = own_part(i, far_k + step)
-        if step > 1:
-            rs["r", i, step - 1].wait_recv()
-            value = value + rs_recv[i, slot - 1].astype(F32)
+    def send_sum(i, slot, value, shift):
         rs_send[i, slot] = value.astype(BF16)
-        rs["r", i, step] = go(remote(rs_send.at[i, slot], rs_recv.at[i, slot],
-                                     rs_ssem.at[i, slot], rs_rsem.at[i, slot], seq=right))
-
-    def rs_step(i, step):
-        if step == 1:
-            answers(i, 1)
-        if step == 3:
-            answers(i, 0)
-        if step <= far_k:
-            rs_left(i, step)
-        if step < far_k:
-            rs_right(i, step)
-        if step == far_k + 1:
-            rs["l", i, far_k].wait_recv()
-            rs["r", i, far_k - 1].wait_recv()
-            total = (own_part(i, 0) + rs_recv[i, far_k - 1].astype(F32) + rs_recv[i, ZS - 2].astype(F32)).astype(BF16)
+        rs[i, slot] = go(remote(rs_send.at[i, slot], rs_recv.at[i, slot], rs_ssem.at[i, slot], rs_rsem.at[i, slot],
+                                seq=seq_id(x, (z + shift) % ZS, c)))
+
+    def far_rows(i):
+        answers(i, 1)
+        send_sum(i, 0, own_part(i, 4), ZS - 1)
+        send_sum(i, 1, own_part(i, 5), 1)
+
+    def far_sums(i):
+        rs[i, 0].wait_recv()
+        send_sum(i, 2, own_part(i, 3) + rs_recv[i, 0].astype(F32), ZS - 3)
+        rs[i, 1].wait_recv()
+        send_sum(i, 3, own_part(i, 6) + rs_recv[i, 1].astype(F32), 2)
+
+    def near_rows(i):
+        answers(i, 0)
+        send_sum(i, 4, own_part(i, 2), ZS - 2)
+        send_sum(i, 5, own_part(i, 1), ZS - 1)
+        send_sum(i, 6, own_part(i, 7), 1)
+
+    def finish(i):
+        total = own_part(i, 0)
+        for slot in range(2, ZS - 1):
+            rs[i, slot].wait_recv()
+            total = total + rs_recv[i, slot].astype(F32)
+        total = total.astype(BF16)
+        if i < NC - PER_Y:
             mine[i] = total
-            if i < NC - PER_Y:
-                peer = (y + 1 + i // PER_Y) % YS
-                rs["y", i] = go(remote(mine.at[i], moe.at[y, i % PER_Y], fy_send.at[i], fy_recv.at[i], exp=peer))
-            else:
-                moe[y, i % PER_Y] = total
-
-    spacing = 8.8 / NC
+            peer = (y + 1 + i // PER_Y) % YS
+            rs["y", i] = go(remote(mine.at[i], moe.at[y, i % PER_Y], fy_send.at[i], fy_recv.at[i], exp=peer))
+        else:
+            moe[y, i % PER_Y] = total
+
+    half_time = 8.8
+    spacing = half_time / NC
     events = []
     for i in range(NC):
-        first, second = spacing * (i + 1), spacing * (NC + i + 1)
-        for step, when in ((1, first), (2, first + 2.8), (3, second), (4, second + 2.8), (5, second + 5.6)):
-            events.append((when, i, step))
-    for when, i, step in sorted(events):
-        rs_step(i, step)
+        far_at = half_time / 2 + spacing * (i + 1)
+        near_at = spacing * (i + 1) if i < NC // 2 else half_time + spacing * (i + 1)
+        events.append((near_at, i, near_rows))
+        events.append((far_at, i, far_rows))
+        events.append((far_at + 2.8, i, far_sums))
+        events.append((max(far_at + 6.7, near_at + 3.2), i, finish))
+    for when, i, act_on in sorted(events, key=lambda event: event[:2]):
+        act_on(i)
 
     for i in range(NC - PER_Y):
         rs["y", i].wait_recv()
@@ -416,8 +420,8 @@
             pltpu.VMEM((NC, ZS, SUB, CW), BF16),
             pltpu.VMEM((NC, 2, XS * CS, GROUP, CW), BF16),
             pltpu.VMEM((NC, 2, XS * CS, GROUP, CW), BF16),
-            pltpu.VMEM((2 * FF // TILE, ROWS, TILE), F32),
-            pltpu.VMEM((ROWS, FF), BF16),
+            pltpu.VMEM((2, 2 * FF // TILE, HROWS, TILE), F32),
+            pltpu.VMEM((2, HROWS, FF), BF16),
             pltpu.VMEM((NC, 2, XS * CS, GROUP, CW), BF16),
             pltpu.VMEM((NC, 2, XS * CS, GROUP, CW), BF16),
             pltpu.VMEM((NC, 2, HALF, SUB, CW), F32),

time: 95.4 us -> 91 us (0.954)
  Pallas kernels: 93.7 us -> 89.3 us
    pallas_call x1, Pallas kernels: 93.7 us -> 89.3 us  [per_device(): pl.pallas_call(layer_kernel, out_shape=jax.ShapeDtypeStruct(residual.shap...]
where the time goes in v3:
time: 91 us; the launch traced here: 90.9 us
  Pallas kernels  89.3 us (98%)
  local copies, waits for them, and re-layouts  1.57 us (2%)
    pallas_call x1, Pallas kernels, per_device(): pl.pallas_call(layer_kernel, out_shape=jax.ShapeDtypeStruct(residual.shap...  89.3 us

profile of v3, /device:TPU:6, one launch (start us, length us, event | category | flops | bytes accessed | tf_op | source)
XLA Modules:
  0.0 90.9 jit_solution(12591944163711914083)
XLA Ops:
  0.0 89.3 %layer.1 = bf16[128,512]{1,0:T(8,128)(2,1)} custom-call(bf16[128,512]{1,0:T(8,128)(2,1)} %q_ref.1, bf16[128,512]{1,0:T(8,128)(2,1)} %k_ref.1, bf16[128,512]{1,0:T(8,128)(2,1)} %v_ref.1, bf16[128,512]{1,0:T(8,128)(2,1)} %res_ref.1, f32[1,512]{1,0:T(1,128)} %bitcast.7, f32[1,2048]{1,0:T(1,128)} %bitcast.4, s32[8,128]{1,0:T(8,128)} %bitcast.5, ...), custom_call_target="tpu_custom_call" | custom-call | tf_op jit(solution)/shard_map/layer/pallas_call | solution.py:401
  89.3 1.6 %copy.12 = bf16[128,512]{1,0:T(8,128)(2,1)} copy(bf16[128,512]{1,0:T(8,128)(2,1)} %layer.1) | data formatting | bytes 262144

commit v4 on v3

--- a/solution.py
+++ b/solution.py
@@ -26,7 +26,15 @@
 HROWS = XS * CS * GROUP
 ROWS = 2 * HROWS
 TILE = 256
-PEERS = ((2, 0), (2, 1), (1, 0), (3, 0), (1, 1), (3, 1), (0, 1))
+PEERS = ((1, 0), (3, 0), (1, 1), (3, 1), (2, 0), (2, 1), (0, 1))
+DIRECT = (True, True, False, False)
+HOPS_RIGHT = (3, 3, 4, 3)
+CHAIN_LEFT = {4: 3, 3: 2, 2: 1, 1: 0, 5: 6, 6: 7, 7: 0}
+CHAIN_RIGHT = {4: 5, 5: 6, 6: 7, 7: 0, 3: 2, 2: 1, 1: 0}
+SHORT_LEFT = {4: 3, 3: 0, 5: 6, 6: 0, 2: 0, 1: 0, 7: 0}
+SHORT_RIGHT = {4: 5, 5: 6, 6: 0, 3: 0, 2: 0, 1: 0, 7: 0}
+TREES = (CHAIN_LEFT, CHAIN_RIGHT, SHORT_RIGHT, SHORT_LEFT)
+EARLY = 2
 
 
 def nt(a, b):
@@ -232,15 +240,25 @@
         ag["l", q, k] = go(remote(blk.at[q, at(ZS - k + 1)], blk.at[q, at(ZS - k)], ag_send.at[q, ZS - k - 1],
                                   ag_recv.at[q, ZS - k - 1], seq=left))
 
-    def ag_step(q, k):
-        if k > 0:
+    def ag_begin(q):
+        ag_right(q, 1)
+        ag_left(q, 1)
+        if DIRECT[q]:
+            ag["r", q, 2] = go(remote(blk.at[q, at(0)], blk.at[q, at(2)], ag_send.at[q, 1], ag_recv.at[q, 1],
+                                      seq=seq_id(x, (z + 2) % ZS, c)))
+
+    def ag_from_left(q, k):
+        if k <= HOPS_RIGHT[q]:
             ag["r", q, k].wait_recv()
-        if k < far_k:
-            ag_right(q, k + 1)
-        if 0 < k < far_k:
+            if k < HOPS_RIGHT[q] and not (DIRECT[q] and k == 1):
+                ag_right(q, k + 1)
+
+    def ag_from_right(q, k):
+        hops = ZS - 1 - HOPS_RIGHT[q]
+        if k <= hops:
             ag["l", q, k].wait_recv()
-        if k + 1 < far_k:
-            ag_left(q, k + 1)
+            if k < hops:
+                ag_left(q, k + 1)
 
     xs = {}
 
@@ -296,11 +314,15 @@
         rt[i, hf, "own"] = own
 
     for q in range(NC):
-        ag_step(q, 0)
+        ag_begin(q)
     for k in range(1, far_k + 1):
         for q in range(NC):
-            ag_step(q, k)
-            if k == 2:
+            if not (DIRECT[q] and k == 2):
+                ag_from_left(q, k)
+            ag_from_right(q, k)
+            if DIRECT[q] and k == 1:
+                ag_from_left(q, 2)
+            if k == (1 if DIRECT[q] else 2):
                 select(q, 0)
             if k == far_k:
                 select(q, 1)
@@ -308,14 +330,14 @@
         expert_up(q, 0)
     activate(0)
     pltpu.make_async_copy(w2, w2, w_sem.at[1]).wait()
-    for i in range(NC // 2):
+    for i in range(EARLY):
         expert_down(i, 0)
     for q in range(NC):
         expert_up(q, 1)
     activate(1)
     for i in range(NC):
         expert_down(i, 1)
-    for i in range(NC // 2, NC):
+    for i in range(EARLY, NC):
         expert_down(i, 0)
 
     rs = {}
@@ -330,34 +352,22 @@
     def own_part(i, k):
         return part[i, at(k) // HALF, at(k) % HALF]
 
-    def send_sum(i, slot, value, shift):
-        rs_send[i, slot] = value.astype(BF16)
-        rs[i, slot] = go(remote(rs_send.at[i, slot], rs_recv.at[i, slot], rs_ssem.at[i, slot], rs_rsem.at[i, slot],
-                                seq=seq_id(x, (z + shift) % ZS, c)))
-
-    def far_rows(i):
-        answers(i, 1)
-        send_sum(i, 0, own_part(i, 4), ZS - 1)
-        send_sum(i, 1, own_part(i, 5), 1)
-
-    def far_sums(i):
-        rs[i, 0].wait_recv()
-        send_sum(i, 2, own_part(i, 3) + rs_recv[i, 0].astype(F32), ZS - 3)
-        rs[i, 1].wait_recv()
-        send_sum(i, 3, own_part(i, 6) + rs_recv[i, 1].astype(F32), 2)
-
-    def near_rows(i):
-        answers(i, 0)
-        send_sum(i, 4, own_part(i, 2), ZS - 2)
-        send_sum(i, 5, own_part(i, 1), ZS - 1)
-        send_sum(i, 6, own_part(i, 7), 1)
+    def gathered_sum(i, k):
+        total = own_part(i, k)
+        for child, parent in TREES[i].items():
+            if parent == k:
+                rs[i, child].wait_recv()
+                total = total + rs_recv[i, child - 1].astype(F32)
+        return total.astype(BF16)
+
+    def pass_on(i, k):
+        rs_send[i, k - 1] = gathered_sum(i, k)
+        target = seq_id(x, (z + TREES[i][k] - k + ZS) % ZS, c)
+        rs[i, k] = go(remote(rs_send.at[i, k - 1], rs_recv.at[i, k - 1], rs_ssem.at[i, k - 1], rs_rsem.at[i, k - 1],
+                             seq=target))
 
     def finish(i):
-        total = own_part(i, 0)
-        for slot in range(2, ZS - 1):
-            rs[i, slot].wait_recv()
-            total = total + rs_recv[i, slot].astype(F32)
-        total = total.astype(BF16)
+        total = gathered_sum(i, 0)
         if i < NC - PER_Y:
             mine[i] = total
             peer = (y + 1 + i // PER_Y) % YS
@@ -365,18 +375,28 @@
         else:
             moe[y, i % PER_Y] = total
 
-    half_time = 8.8
+    half_time, hop_time = 8.8, 2.8
     spacing = half_time / NC
     events = []
     for i in range(NC):
-        far_at = half_time / 2 + spacing * (i + 1)
-        near_at = spacing * (i + 1) if i < NC // 2 else half_time + spacing * (i + 1)
-        events.append((near_at, i, near_rows))
-        events.append((far_at, i, far_rows))
-        events.append((far_at + 2.8, i, far_sums))
-        events.append((max(far_at + 6.7, near_at + 3.2), i, finish))
-    for when, i, act_on in sorted(events, key=lambda event: event[:2]):
-        act_on(i)
+        far_at = half_time * EARLY / NC + spacing * (i + 1)
+        near_at = spacing * (i + 1) if i < EARLY else half_time + spacing * (i + 1)
+        events.append((near_at, i, 0, functools.partial(answers, i, 0)))
+        events.append((far_at, i, 0, functools.partial(answers, i, 1)))
+        sent_at = {}
+
+        def ready(k):
+            if k not in sent_at:
+                held = near_at if k in (7, 0, 1, 2) else far_at
+                waits = [ready(child) + hop_time for child, parent in TREES[i].items() if parent == k]
+                sent_at[k] = max([held] + waits)
+            return sent_at[k]
+
+        for k in range(1, ZS):
+            events.append((ready(k), i, 1, functools.partial(pass_on, i, k)))
+        events.append((ready(0), i, 2, functools.partial(finish, i)))
+    for event in sorted(events, key=lambda event: event[:3]):
+        event[3]()
 
     for i in range(NC - PER_Y):
         rs["y", i].wait_recv()

time: 91 us -> 93.5 us (1.027)
  Pallas kernels: 89.3 us -> 91 us
    pallas_call x1, Pallas kernels: 89.3 us -> 91 us  [per_device(): pl.pallas_call(layer_kernel, out_shape=jax.ShapeDtypeStruct(residual.shap...]
where the time goes in v4:
time: 93.5 us; the launch traced here: 92.6 us
  Pallas kernels  91 us (97%)
  local copies, waits for them, and re-layouts  1.57 us (2%)
    pallas_call x1, Pallas kernels, per_device(): pl.pallas_call(layer_kernel, out_shape=jax.ShapeDtypeStruct(residual.shap...  91 us

profile of v4, /device:TPU:6, one launch (start us, length us, event | category | flops | bytes accessed | tf_op | source)
XLA Modules:
  0.0 92.6 jit_solution(7195197220636137896)
XLA Ops:
  0.0 91.0 %layer.1 = bf16[128,512]{1,0:T(8,128)(2,1)} custom-call(bf16[128,512]{1,0:T(8,128)(2,1)} %q_ref.1, bf16[128,512]{1,0:T(8,128)(2,1)} %k_ref.1, bf16[128,512]{1,0:T(8,128)(2,1)} %v_ref.1, bf16[128,512]{1,0:T(8,128)(2,1)} %res_ref.1, f32[1,512]{1,0:T(1,128)} %bitcast.7, f32[1,2048]{1,0:T(1,128)} %bitcast.4, s32[8,128]{1,0:T(8,128)} %bitcast.5, ...), custom_call_target="tpu_custom_call" | custom-call | tf_op jit(solution)/shard_map/layer/pallas_call | solution.py:421
  91.0 1.6 %copy.12 = bf16[128,512]{1,0:T(8,128)(2,1)} copy(bf16[128,512]{1,0:T(8,128)(2,1)} %layer.1) | data formatting | bytes 262144

commit v5 on v3

--- a/solution.py
+++ b/solution.py
@@ -14,6 +14,8 @@
 HEAD = 128
 XS, ZS, CS, YS = 4, 8, 2, 4
 SEQ = XS * ZS * CS
+SLAB = ZS * CS
+PIECE = 512 // SLAB
 D = 2048
 FF = 1024
 SUB = 32
@@ -26,7 +28,7 @@
 HROWS = XS * CS * GROUP
 ROWS = 2 * HROWS
 TILE = 256
-PEERS = ((2, 0), (2, 1), (1, 0), (3, 0), (1, 1), (3, 1), (0, 1))
+PEERS = ((1, 0), (3, 0), (1, 1), (3, 1), (2, 0), (2, 1), (0, 1))
 
 
 def nt(a, b):
@@ -49,9 +51,9 @@
 def layer_kernel(
     q_ref, k_ref, v_ref, res_ref, hgain_ref, ngain_ref, routes_ref, gates_ref, win_ref, wout_ref,
     out_ref,
-    w1, w2, state, gathered, running, prior, raw, hidden, rows, meta, place, mixhi, mixlo,
+    w1, w2, state, gathered, running, prior, totals, raw, hidden, rows, meta, place, mixhi, mixlo,
     blk, sel, xin, acc, act, yout, ret, part, rs_send, rs_recv, mine, moe,
-    w_sem, st_send, st_recv, pr_send, pr_recv, meta_send, meta_recv, y_send, y_recv,
+    w_sem, st_send, st_recv, tot_send, tot_recv, pr_send, pr_recv, meta_send, meta_recv, y_send, y_recv,
     ag_send, ag_recv, xs_send, xs_recv, loc_sem, rt_send, rt_recv, rs_ssem, rs_rsem, fy_send, fy_recv,
 ):
     me = lax.axis_index("seq")
@@ -91,31 +93,32 @@
 
     barrier = pltpu.get_barrier_semaphore()
 
-    def greet(i, _):
-        pl.semaphore_signal(barrier, inc=1, device_id=((me + i) % SEQ, y), device_id_type=MESH)
-        return 0
-
-    lax.fori_loop(1, SEQ, greet, 0)
+    place_in_slab = me % SLAB
+    shifts = [SLAB // 2] + [shift for i in range(SLAB // 2 - 1, 0, -1) for shift in (i, SLAB - i)]
+    slab_peers = [(x * SLAB + (place_in_slab + shift) % SLAB, (place_in_slab + shift) % SLAB) for shift in shifts]
+
+    def greet(peer, other=None):
+        pl.semaphore_signal(barrier, inc=1, device_id=(peer, y if other is None else other), device_id_type=MESH)
+
+    for peer, _ in slab_peers:
+        greet(peer)
+    for dx, dc in PEERS:
+        if dx:
+            greet(seq_id((x + dx) % XS, z, (c + dc) % CS))
     for j in range(1, YS):
-        pl.semaphore_signal(barrier, inc=1, device_id=(me, (y + j) % YS), device_id_type=MESH)
+        greet(me, (y + j) % YS)
+    greeted = SLAB - 1 + (XS - 1) * CS + YS - 1
 
     heads = q_ref.shape[1] // HEAD
     for h in range(heads):
         cols = pl.ds(h * HEAD, HEAD)
         outer = tn(k_ref[:, cols], v_ref[:, cols])
-        state[pl.ds(h * 16, 16)] = outer.reshape(16, 8, HEAD).astype(BF16)
-
-    pl.semaphore_wait(barrier, SEQ - 1 + YS - 1)
-
-    def send_state(i, _):
-        for peer in ((me + i) % SEQ, (me + SEQ - i) % SEQ):
-            remote(state.at[peer], gathered.at[me], st_send, st_recv, seq=peer).start()
-        return 0
-
-    lax.fori_loop(1, SEQ // 2, send_state, 0)
-    far = (me + SEQ // 2) % SEQ
-    remote(state.at[far], gathered.at[me], st_send, st_recv, seq=far).start()
-    gathered[me] = state[me]
+        state[pl.ds(h * HEAD // PIECE, HEAD // PIECE)] = outer.reshape(HEAD // PIECE, PIECE, HEAD).astype(BF16)
+
+    pl.semaphore_wait(barrier, greeted)
+    for peer, where in slab_peers:
+        remote(state.at[where], gathered.at[place_in_slab], st_send, st_recv, seq=peer).start()
+    gathered[place_in_slab] = state[place_in_slab]
 
     tok = lax.broadcasted_iota(jnp.int32, (128, 128), 1)
     row = lax.broadcasted_iota(jnp.int32, (128, 128), 0)
@@ -144,24 +147,29 @@
         raw[:, cols] = nn(high, v_ref[:, cols]) + nn(low, v_ref[:, cols])
 
     def others(ref):
-        return ref.at[pl.ds(0, SEQ - 1)]
+        return ref.at[pl.ds(0, SLAB - 1)]
 
     remote(others(state), others(gathered), st_send, st_recv).wait_recv()
 
-    def scan_step(s, total):
-        running[s] = total.astype(BF16)
-        return total + gathered[s].astype(F32)
-
-    lax.fori_loop(0, SEQ, scan_step, jnp.zeros((8, HEAD), F32))
-
-    def send_prior(i, _):
-        for peer in ((me + i) % SEQ, (me + SEQ - i) % SEQ):
-            remote(running.at[peer], prior.at[me], pr_send, pr_recv, seq=peer).start()
-        return 0
-
-    lax.fori_loop(1, SEQ // 2, send_prior, 0)
-    remote(running.at[far], prior.at[me], pr_send, pr_recv, seq=far).start()
-    prior[me] = running[me]
+    total = jnp.zeros((PIECE, HEAD), F32)
+    for g in range(SLAB):
+        total = total + gathered[g].astype(F32)
+    totals[x] = total
+    slab_copies = []
+    for dx in (2, 1, 3):
+        slab_copies.append(go(remote(totals.at[x], totals.at[x], tot_send.at[dx - 1], tot_recv.at[dx - 1],
+                                     seq=seq_id((x + dx) % XS, z, c))))
+    for copy in slab_copies:
+        copy.wait_recv()
+    total = jnp.zeros((PIECE, HEAD), F32)
+    for xx in range(XS):
+        total = total + jnp.where(xx < x, totals[xx], 0.0)
+    for g in range(SLAB):
+        running[g] = total.astype(BF16)
+        total = total + gathered[g].astype(F32)
+    for peer, where in slab_peers:
+        remote(running.at[where], prior.at[place_in_slab], pr_send, pr_recv, seq=peer).start()
+    prior[place_in_slab] = running[place_in_slab]
 
     for copy in pending[:ZS - 1]:
         copy.wait_recv()
@@ -195,7 +203,7 @@
     remote(others(running), others(prior), pr_send, pr_recv).wait_recv()
     for h in range(heads):
         cols = pl.ds(h * HEAD, HEAD)
-        before = prior[pl.ds(h * 16, 16)].astype(F32).reshape(HEAD, HEAD).astype(BF16)
+        before = prior[pl.ds(h * HEAD // PIECE, HEAD // PIECE)].reshape(HEAD, HEAD)
         total = nn(q_ref[:, cols], before) + raw[:, cols]
         scale = lax.rsqrt(jnp.mean(total * total, axis=1, keepdims=True) + 1e-6)
         hidden[:, cols] = (res_ref[:, cols].astype(F32) + total * scale * hgain_ref[:, cols]).astype(BF16)
@@ -406,10 +414,11 @@
         scratch_shapes=[
             pltpu.VMEM((2, NC, CW, FF), BF16),
             pltpu.VMEM((NC, FF, CW), BF16),
-            pltpu.VMEM((SEQ, 8, HEAD), BF16),
-            pltpu.VMEM((SEQ, 8, HEAD), BF16),
-            pltpu.VMEM((SEQ, 8, HEAD), BF16),
-            pltpu.VMEM((SEQ, 8, HEAD), BF16),
+            pltpu.VMEM((SLAB, PIECE, HEAD), BF16),
+            pltpu.VMEM((SLAB, PIECE, HEAD), BF16),
+            pltpu.VMEM((SLAB, PIECE, HEAD), BF16),
+            pltpu.VMEM((SLAB, PIECE, HEAD), BF16),
+            pltpu.VMEM((XS, PIECE, HEAD), F32),
             pltpu.VMEM(residual.shape, F32),
             pltpu.VMEM(residual.shape, BF16),
             pltpu.VMEM((YS, SUB, D // YS), BF16),
@@ -429,7 +438,7 @@
             pltpu.VMEM((NC, ZS - 1, SUB, CW), BF16),
             pltpu.VMEM((NC, SUB, CW), BF16),
             pltpu.VMEM((YS, PER_Y, SUB, CW), BF16),
-            dma((2,)), dma, dma, dma, dma,
+            dma((2,)), dma, dma, dma((XS - 1,)), dma((XS - 1,)), dma, dma,
             dma((ZS - 1,)), dma((ZS - 1,)),
             dma((YS - 1,)), dma((YS - 1,)),
             dma((NC, ZS - 1)), dma((NC, ZS - 1)),

time: 91 us -> 88.5 us (0.973); the launches traced: 90.9 us -> 87.5 us
  Pallas kernels: 89.3 us -> 85.9 us
    pallas_call x1, Pallas kernels: 89.3 us -> 85.9 us  [per_device(): pl.pallas_call(layer_kernel, out_shape=jax.ShapeDtypeStruct(residual.shap...]
where the time goes in v5:
time: 88.5 us; the launch traced here: 87.5 us
  Pallas kernels  85.9 us (97%)
  local copies, waits for them, and re-layouts  1.57 us (2%)
    pallas_call x1, Pallas kernels, per_device(): pl.pallas_call(layer_kernel, out_shape=jax.ShapeDtypeStruct(residual.shap...  85.9 us

profile of v5, /device:TPU:6, one launch (start us, length us, event | category | flops | bytes accessed | tf_op | source)
XLA Modules:
  0.0 87.5 jit_solution(9250417770648116905)
XLA Ops:
  0.0 85.9 %layer.1 = bf16[128,512]{1,0:T(8,128)(2,1)} custom-call(bf16[128,512]{1,0:T(8,128)(2,1)} %q_ref.1, bf16[128,512]{1,0:T(8,128)(2,1)} %k_ref.1, bf16[128,512]{1,0:T(8,128)(2,1)} %v_ref.1, bf16[128,512]{1,0:T(8,128)(2,1)} %res_ref.1, f32[1,512]{1,0:T(1,128)} %bitcast.7, f32[1,2048]{1,0:T(1,128)} %bitcast.4, s32[8,128]{1,0:T(8,128)} %bitcast.5, ...), custom_call_target="tpu_custom_call" | custom-call | tf_op jit(solution)/shard_map/layer/pallas_call | solution.py:409
  85.9 1.6 %copy.12 = bf16[128,512]{1,0:T(8,128)(2,1)} copy(bf16[128,512]{1,0:T(8,128)(2,1)} %layer.1) | data formatting | bytes 262144

commit v6 on v5

--- a/solution.py
+++ b/solution.py
@@ -29,6 +29,12 @@
 ROWS = 2 * HROWS
 TILE = 256
 PEERS = ((1, 0), (3, 0), (1, 1), (3, 1), (2, 0), (2, 1), (0, 1))
+HOPS_RIGHT = (4, 3, 4, 3)
+SHORT_LEFT = {4: 3, 3: 0, 5: 6, 6: 0, 2: 0, 1: 0, 7: 0}
+TREES = (SHORT_LEFT,) * 4
+PIECES = ((0, 0), (1, 0), (0, 1), (1, 1), (2, 1), (3, 1), (2, 0), (3, 0))
+EARLY = 2
+WINDOW = 4
 
 
 def nt(a, b):
@@ -215,6 +221,26 @@
             hidden.at[pl.ds(pl.multiple_of(peer * SUB, SUB), SUB), :], rows.at[y],
             y_send.at[j - 1], y_recv.at[j - 1], exp=peer)))
     rows[y] = hidden[pl.ds(pl.multiple_of(y * SUB, SUB), SUB), :]
+    right = seq_id(x, (z + 1) % ZS, c)
+    left = seq_id(x, (z + ZS - 1) % ZS, c)
+    far_k = ZS // 2
+    ag = {}
+
+    def at(k):
+        return (k + 1) % ZS
+
+    def ag_right(q, k):
+        ag["r", q, k] = go(remote(blk.at[q, at(k - 1)], blk.at[q, at(k)], ag_send.at[q, k - 1],
+                                  ag_recv.at[q, k - 1], seq=right))
+
+    def ag_left(q, k):
+        ag["l", q, k] = go(remote(blk.at[q, at(ZS - k + 1)], blk.at[q, at(ZS - k)], ag_send.at[q, ZS - k - 1],
+                                  ag_recv.at[q, ZS - k - 1], seq=left))
+
+    def ag_begin(q):
+        ag_right(q, 1)
+        ag_left(q, 1)
+
     for copy in y_copies:
         copy.wait_recv()
     wide = [rows[j].astype(F32) for j in range(YS)]
@@ -223,32 +249,20 @@
     for q in range(NC):
         part_cols = wide[q // PER_Y][:, (q % PER_Y) * CW:(q % PER_Y + 1) * CW]
         blk[q, 1] = (part_cols * scale * ngain_ref[:, q * CW:(q + 1) * CW]).astype(BF16)
-
-    right = seq_id(x, (z + 1) % ZS, c)
-    left = seq_id(x, (z + ZS - 1) % ZS, c)
-    far_k = ZS // 2
-    ag = {}
-
-    def at(k):
-        return (k + 1) % ZS
-
-    def ag_right(q, k):
-        ag["r", q, k] = go(remote(blk.at[q, at(k - 1)], blk.at[q, at(k)], ag_send.at[q, k - 1],
-                                  ag_recv.at[q, k - 1], seq=right))
-
-    def ag_left(q, k):
-        ag["l", q, k] = go(remote(blk.at[q, at(ZS - k + 1)], blk.at[q, at(ZS - k)], ag_send.at[q, ZS - k - 1],
-                                  ag_recv.at[q, ZS - k - 1], seq=left))
-
-    def ag_step(q, k):
-        if k > 0:
+        ag_begin(q)
+
+    def ag_from_left(q, k):
+        if k <= HOPS_RIGHT[q]:
             ag["r", q, k].wait_recv()
-        if k < far_k:
-            ag_right(q, k + 1)
-        if 0 < k < far_k:
+            if k < HOPS_RIGHT[q]:
+                ag_right(q, k + 1)
+
+    def ag_from_right(q, k):
+        hops = ZS - 1 - HOPS_RIGHT[q]
+        if k <= hops:
             ag["l", q, k].wait_recv()
-        if k + 1 < far_k:
-            ag_left(q, k + 1)
+            if k < hops:
+                ag_left(q, k + 1)
 
     xs = {}
 
@@ -295,6 +309,8 @@
             cols = pl.ds(n * TILE, TILE)
             value = nn(act[hf], w2[order[i], :, cols]).astype(BF16)
             yout[i, hf, :, :, cols] = value.reshape(XS * CS, GROUP, TILE)
+
+    def send_back(i, hf):
         for j, (dx, dc) in enumerate(PEERS):
             xx, cc = (x + dx) % XS, (c + dc) % CS
             rt[i, hf, j] = go(remote(yout.at[i, hf, xx * CS + cc], ret.at[i, hf, mine_d], rt_send.at[i, hf, j],
@@ -303,11 +319,10 @@
         own.start()
         rt[i, hf, "own"] = own
 
-    for q in range(NC):
-        ag_step(q, 0)
     for k in range(1, far_k + 1):
         for q in range(NC):
-            ag_step(q, k)
+            ag_from_left(q, k)
+            ag_from_right(q, k)
             if k == 2:
                 select(q, 0)
             if k == far_k:
@@ -316,15 +331,23 @@
         expert_up(q, 0)
     activate(0)
     pltpu.make_async_copy(w2, w2, w_sem.at[1]).wait()
-    for i in range(NC // 2):
-        expert_down(i, 0)
+    way_out = list(pending)
+    pending.clear()
+    for i, hf in PIECES[:EARLY]:
+        expert_down(i, hf)
+        send_back(i, hf)
     for q in range(NC):
         expert_up(q, 1)
     activate(1)
-    for i in range(NC):
-        expert_down(i, 1)
-    for i in range(NC // 2, NC):
-        expert_down(i, 0)
+    for n, (i, hf) in enumerate(PIECES):
+        if n >= EARLY:
+            expert_down(i, hf)
+            if n < WINDOW:
+                send_back(i, hf)
+    remote(others(state), others(gathered), st_send, st_recv).wait_send()
+    remote(others(running), others(prior), pr_send, pr_recv).wait_send()
+    for copy in way_out:
+        copy.wait_send()
 
     rs = {}
 
@@ -333,39 +356,30 @@
             rt[i, hf, j].wait_recv()
         rt[i, hf, "own"].wait()
         value = ret[i, hf].reshape(HROWS, CW)
+        later = PIECES.index((i, hf)) + WINDOW
+        if later < len(PIECES):
+            send_back(*PIECES[later])
         part[i, hf] = (nn(mixhi[hf], value) + nn(mixlo[hf], value)).reshape(HALF, SUB, CW)
 
     def own_part(i, k):
         return part[i, at(k) // HALF, at(k) % HALF]
 
-    def send_sum(i, slot, value, shift):
-        rs_send[i, slot] = value.astype(BF16)
-        rs[i, slot] = go(remote(rs_send.at[i, slot], rs_recv.at[i, slot], rs_ssem.at[i, slot], rs_rsem.at[i, slot],
-                                seq=seq_id(x, (z + shift) % ZS, c)))
-
-    def far_rows(i):
-        answers(i, 1)
-        send_sum(i, 0, own_part(i, 4), ZS - 1)
-        send_sum(i, 1, own_part(i, 5), 1)
-
-    def far_sums(i):
-        rs[i, 0].wait_recv()
-        send_sum(i, 2, own_part(i, 3) + rs_recv[i, 0].astype(F32), ZS - 3)
-        rs[i, 1].wait_recv()
-        send_sum(i, 3, own_part(i, 6) + rs_recv[i, 1].astype(F32), 2)
-
-    def near_rows(i):
-        answers(i, 0)
-        send_sum(i, 4, own_part(i, 2), ZS - 2)
-        send_sum(i, 5, own_part(i, 1), ZS - 1)
-        send_sum(i, 6, own_part(i, 7), 1)
+    def gathered_sum(i, k):
+        total = own_part(i, k)
+        for child, parent in TREES[i].items():
+            if parent == k:
+                rs[i, child].wait_recv()
+                total = total + rs_recv[i, child - 1].astype(F32)
+        return total.astype(BF16)
+
+    def pass_on(i, k):
+        rs_send[i, k - 1] = gathered_sum(i, k)
+        target = seq_id(x, (z + TREES[i][k] - k + ZS) % ZS, c)
+        rs[i, k] = go(remote(rs_send.at[i, k - 1], rs_recv.at[i, k - 1], rs_ssem.at[i, k - 1], rs_rsem.at[i, k - 1],
+                             seq=target))
 
     def finish(i):
-        total = own_part(i, 0)
-        for slot in range(2, ZS - 1):
-            rs[i, slot].wait_recv()
-            total = total + rs_recv[i, slot].astype(F32)
-        total = total.astype(BF16)
+        total = gathered_sum(i, 0)
         if i < NC - PER_Y:
             mine[i] = total
             peer = (y + 1 + i // PER_Y) % YS
@@ -373,18 +387,28 @@
         else:
             moe[y, i % PER_Y] = total
 
-    half_time = 8.8
+    half_time, hop_time = 8.8, 2.8
     spacing = half_time / NC
     events = []
     for i in range(NC):
-        far_at = half_time / 2 + spacing * (i + 1)
-        near_at = spacing * (i + 1) if i < NC // 2 else half_time + spacing * (i + 1)
-        events.append((near_at, i, near_rows))
-        events.append((far_at, i, far_rows))
-        events.append((far_at + 2.8, i, far_sums))
-        events.append((max(far_at + 6.7, near_at + 3.2), i, finish))
-    for when, i, act_on in sorted(events, key=lambda event: event[:2]):
-        act_on(i)
+        near_at = spacing * (PIECES.index((i, 0)) + 1)
+        far_at = spacing * (PIECES.index((i, 1)) + 1)
+        events.append((near_at, i, 0, functools.partial(answers, i, 0)))
+        events.append((far_at, i, 0, functools.partial(answers, i, 1)))
+        sent_at = {}
+
+        def ready(k):
+            if k not in sent_at:
+                held = near_at if k in (7, 0, 1, 2) else far_at
+                waits = [ready(child) + hop_time for child, parent in TREES[i].items() if parent == k]
+                sent_at[k] = max([held] + waits)
+            return sent_at[k]
+
+        for k in range(1, ZS):
+            events.append((ready(k), i, 1, functools.partial(pass_on, i, k)))
+        events.append((ready(0), i, 2, functools.partial(finish, i)))
+    for event in sorted(events, key=lambda event: event[:3]):
+        event[3]()
 
     for i in range(NC - PER_Y):
         rs["y", i].wait_recv()
@@ -394,8 +418,6 @@
             sub = pl.ds(j * SUB, SUB)
             out_ref[sub, cols] = (hidden[sub, cols].astype(F32) + moe[j, p].astype(F32)).astype(BF16)
 
-    remote(others(state), others(gathered), st_send, st_recv).wait_send()
-    remote(others(running), others(prior), pr_send, pr_recv).wait_send()
     for copy in pending:
         copy.wait_send()
 

time: 88.5 us -> 88.2 us (level)
  no operation moved by 1% of the time
where the time goes in v6:
time: 88.2 us; the launch traced here: 86.7 us
  Pallas kernels  85.1 us (96%)
  local copies, waits for them, and re-layouts  1.57 us (2%)
    pallas_call x1, Pallas kernels, per_device(): pl.pallas_call(layer_kernel, out_shape=jax.ShapeDtypeStruct(residual.shap...  85.1 us

profile of v6, /device:TPU:6, one launch (start us, length us, event | category | flops | bytes accessed | tf_op | source)
XLA Modules:
  0.0 86.7 jit_solution(702338560123287071)
XLA Ops:
  0.0 85.1 %layer.1 = bf16[128,512]{1,0:T(8,128)(2,1)} custom-call(bf16[128,512]{1,0:T(8,128)(2,1)} %q_ref.1, bf16[128,512]{1,0:T(8,128)(2,1)} %k_ref.1, bf16[128,512]{1,0:T(8,128)(2,1)} %v_ref.1, bf16[128,512]{1,0:T(8,128)(2,1)} %res_ref.1, f32[1,512]{1,0:T(1,128)} %bitcast.7, f32[1,2048]{1,0:T(1,128)} %bitcast.4, s32[8,128]{1,0:T(8,128)} %bitcast.5, ...), custom_call_target="tpu_custom_call" | custom-call | tf_op jit(solution)/shard_map/layer/pallas_call | solution.py:431
  85.1 1.6 %copy.12 = bf16[128,512]{1,0:T(8,128)(2,1)} copy(bf16[128,512]{1,0:T(8,128)(2,1)} %layer.1) | data formatting | bytes 262144
